TPU v7x, 32 devices: a whole 2x2x4 slice. The times are simulated.
32 devices in a mesh: survey: 2 (over y), off: 8 (over z, x), gy: 2 (over core).
Axes of the slice: x: 2, y: 2, z: 4, core: 2. Of those that a mesh axis runs over, the one named last changes fastest.
Arguments:
- checkpoint: float32 [16, 2, 2, 16, 48, 256], P(('survey', 'off'), None, None, 'gy'), parts along dimension 0, may hold values from -6 to 6
- traces: float32 [16, 4, 16, 256], P(('survey', 'off'), None, 'gy'), parts along dimension 0, may hold values from -6 to 6
- courant_sq: float32 [16, 48, 256], P('gy'), may hold values from 0.06 to 0.18
- holder: int32 [8], P('survey'), parts along dimension 0, may hold values from 0 to 7, as said below
- offset_lags: int32 [16, 4], P(('survey', 'off')), parts along dimension 0, may hold values from -16 to 15, as said below
Outputs:
- offset_image: float32 [64, 16, 48, 256], P(('survey', 'off'), 'gy'), parts along dimension 0
There are 2 independent parts, one for each index of `survey`. A program takes and returns all parts, laid end to end along the dimension named above; an argument that names none is the same for every part. Nothing has to cross between parts.
Inputs may be any that keep to these rules, and one draw needn't show every extreme that they name: `holder`: the 4 entries are distinct; every draw contains both 0 and 8 - 1. `offset_lags`: each of the 32 values from -16 to 15 appears exactly once.
All inputs are finite; a program needn't handle non-finite values.
Results may differ from a plain program's by a relative error of at most 0.0041.
Values may be sent and summed in bfloat16 or wider, within the bound.
No kernel may reach another device: no remote copies, remote signals or barrier semaphores. Data moves between devices by JAX's collectives and lax.ppermute only.
A program may use at most 128 MiB of HBM per device.

v0:
```python
import jax
import jax.numpy as jnp
from jax import lax
from jax.sharding import PartitionSpec as P

stencil_taps = (-205.0 / 72.0, 8.0 / 5.0, -1.0 / 5.0, 8.0 / 315.0, -1.0 / 560.0)


def extended_2(shard, sides, width):
    for axis, dim in sides:
        devices, length = (lax.axis_size(axis), shard.shape[dim])
        up = [(i, (i + 1) % devices) for i in range(devices - 1)]
        down = [(j, i) for i, j in up]
        last = lax.slice_in_dim(shard, length - width, length, axis=dim)
        initial = lax.slice_in_dim(shard, 0, width, axis=dim)
        before = lax.ppermute(last, axis, up)
        after = lax.ppermute(initial, axis, down)
        shard = jnp.concatenate([before, shard, after], axis=dim)
    return shard


def spread(value, axis, source):
    kept = jnp.where(lax.axis_index(axis) == source, value, 0).astype(value.dtype)
    return lax.psum(kept, axis)


def laplace(extended):
    cells_y = extended.shape[-3] - 8
    cells_z = extended.shape[-2]
    cells_x = extended.shape[-1]
    leading = [(0, 0)] * (extended.ndim - 2)
    padded = jnp.pad(extended, leading + [(4, 4), (4, 4)])

    def shifted(step_y, step_z, step_x):
        return padded[
            ...,
            4 + step_y : 4 + step_y + cells_y,
            4 + step_z : 4 + step_z + cells_z,
            4 + step_x : 4 + step_x + cells_x,
        ]

    summed = 3.0 * stencil_taps[0] * shifted(0, 0, 0)
    for tap_no in range(1, 5):
        beside_all = shifted(tap_no, 0, 0) + shifted(-tap_no, 0, 0)
        beside_all = beside_all + shifted(0, tap_no, 0) + shifted(0, -tap_no, 0)
        beside_all = beside_all + shifted(0, 0, tap_no) + shifted(0, 0, -tap_no)
        summed = summed + stencil_taps[tap_no] * beside_all
    return summed


def propagate_step(earlier, current, courant_sq, drive):
    extended = extended_2(current, (("gy", 2),), 4)
    advanced = 2.0 * current - earlier + courant_sq * laplace(extended)
    advanced = advanced.at[:, 1, :, 0, :].add(drive)
    return (current, advanced)


def correlate(image_acc, source, receiver, my_lags, half_span):
    cells_x = receiver.shape[-1]
    padded = jnp.pad(receiver, ((0, 0), (0, 0), (half_span, half_span)))
    moved = jax.vmap(
        lambda lag_value: lax.dynamic_slice_in_dim(padded, half_span + lag_value, cells_x, 2)
    )(my_lags)
    return image_acc + source.astype(jnp.float32)[None] * moved.astype(jnp.float32)


def on_device(checkpoint, traces, courant_sq, holder, offset_lags):
    shot_count = holder.shape[0]
    step_count = traces.shape[1]
    my_lags = offset_lags[0]
    half_span = lax.axis_size("off") * offset_lags.shape[1] // 2
    image_acc = jnp.zeros((offset_lags.shape[1],) + courant_sq.shape, jnp.float32)
    earlier = checkpoint[:, 0]
    current = checkpoint[:, 1]
    collected = []
    for step_no in range(step_count):
        earlier, current = propagate_step(earlier, current, courant_sq, traces[:, step_no])
        if step_no % 2 == 1:
            snapshot = current[0].astype(jnp.bfloat16)
            collected.append(snapshot)
    snap_runs = jnp.stack(collected)
    for shot_no in range(shot_count):
        received = spread(snap_runs, "off", holder[shot_no])
        for snap_no in range(received.shape[0]):
            image_acc = correlate(
                image_acc, received[snap_no, 0], received[snap_no, 1], my_lags, half_span
            )
    return image_acc


def solution(mesh):
    placed = (
        P(("survey", "off"), None, None, "gy", None, None),
        P(("survey", "off"), None, "gy", None),
        P("gy", None, None),
        P("survey"),
        P(("survey", "off"), None),
    )
    return jax.shard_map(
        on_device,
        mesh=mesh,
        in_specs=placed,
        out_specs=P(("survey", "off"), "gy", None, None),
        check_vma=False,
    )
```

profile of v0, /device:TPU:0, one launch (start us, length us, event | category | flops | bytes accessed | tf_op | source)
XLA Modules:
  0.0 278.0 jit_solution(1497797159843824747)
XLA Ops:
  8.8 2.4 collective-permute-start.1
  16.6 3.6 %fusion.103 = f32[1,2,8,48,256]{4,2,3,1,0:T(8,128)S(1)} fusion(f32[1,2,8,48,256]{4,2,3,1,0:T(8,128)S(1)} %bitcast.98, f32[1,2,4,48,256]{4,2,3,1,0:T(4,128)S(1)} %copy.142, f32[1,2,4,48,256]{4,2,3,1,0:T(4,128)S(1)} %copy.140, f32[1,2,16,56,264]{4,2,3,1,0:T(8,128)S(1)} %select_maximum_fusion.6, f32[1,1,2,8,48,256]{5,4,3,2,1,0:T(8,128)S(1)} %get-tuple-element.57, ...), kind=kLoop, calls=%fused_computation.172 | loop fusion | flops 8060928 | bytes 16121856 | tf_op jit(solution)/shard_map/add | solution.py:53
  28.7 3.6 %fusion.73 = f32[1,2,8,48,256]{4,2,3,1,0:T(8,128)S(1)} fusion(f32[1,2,8,48,256]{4,2,3,1,0:T(8,128)S(1)} %fusion.144, f32[1,2,4,48,256]{4,2,3,1,0:T(4,128)S(1)} %copy.148, f32[1,2,4,48,256]{4,2,3,1,0:T(4,128)S(1)} %copy.146, f32[1,2,16,56,264]{4,2,3,1,0:T(8,128)S(1)} %select_maximum_fusion.4, f32[8,48,256]{2,0,1:T(8,128)S(1)} %copy-done.3, ...), kind=kLoop, calls=%fused_computation.142 | loop fusion | flops 8060928 | bytes 16121856 | tf_op jit(solution)/shard_map/add | solution.py:53
  40.1 3.4 %fusion.43 = f32[1,2,8,48,256]{4,2,3,1,0:T(8,128)S(1)} fusion(f32[1,2,8,48,256]{4,2,3,1,0:T(8,128)S(1)} %fusion.143, f32[1,2,4,48,256]{4,2,3,1,0:T(4,128)S(1)} %copy.154, f32[1,2,4,48,256]{4,2,3,1,0:T(4,128)S(1)} %copy.152, f32[1,2,16,56,264]{4,2,3,1,0:T(8,128)S(1)} %select_maximum_fusion.2, f32[1,2,8,48,256]{4,2,3,1,0:T(8,128)S(1)} %fusion.144, ...), kind=kLoop, calls=%fused_computation.112 | loop fusion | flops 8060928 | bytes 16121856 | tf_op jit(solution)/shard_map/add | solution.py:53
  44.6 2.2 collective-permute-start.7
  53.5 3.7 %fusion.13 = f32[1,2,8,48,256]{4,2,3,1,0:T(8,128)S(1)} fusion(f32[1,2,8,48,256]{4,2,3,1,0:T(8,128)S(1)} %copy-done.1, f32[1,2,4,48,256]{4,2,3,1,0:T(4,128)S(1)} %copy.160, f32[1,2,4,48,256]{4,2,3,1,0:T(4,128)S(1)} %copy.158, f32[1,2,16,56,264]{4,2,3,1,0:T(8,128)S(1)} %select_maximum_fusion, f32[1,2,8,48,256]{4,2,3,1,0:T(8,128)S(1)} %fusion.143, ...), kind=kLoop, calls=%fused_computation.82 | loop fusion | flops 8060928 | bytes 16121856 | tf_op jit(solution)/shard_map/add | solution.py:53
  59.9 131.8 %all-reduce.16.cloned.1.call-done = (bf16[2,2,8,48,256]{4,2,3,1,0:T(8,128)(2,1)}, bf16[2,2,8,48,256]{4,2,3,1,0:T(8,128)(2,1)}, bf16[2,2,8,48,256]{4,2,3,1,0:T(8,128)(2,1)}, bf16[2,2,8,48,256]{4,2,3,1,0:T(8,128)(2,1)}) async-done(((bf16[2,2,8,48,256]{4,2,3,1,0:T(8,128)(2,1)}, bf16[2,2,8,48,256]{4,2,3,1,0:T(8,128)(2,1)}, bf16[2,2,8,48,256]{4,2,3,1,0:T(8,128)(2,1)}, bf16[2,2,8,48,256]{4,2,3,1,0:T(8,128)(2,1)}), ...) | async-done | bytes 3145744 | tf_op jit(solution)/shard_map/psum | solution.py:24
  191.7 2.4 fusion.133
  203.0 3.2 %gather_fusion.5 = bf16[4,8,48,256]{2,1,3,0:T(8,128)(2,1)} fusion(bf16[8,48,288]{1,0,2:T(8,128)(2,1)} %pad.64.clone, s32[4]{0:T(128)S(1)} %shift-left_bitcast_fusion), kind=kCustom, calls=%fused_computation.5 | custom fusion | bytes 1572912 | tf_op jit(solution)/shard_map/vmap()/gather | solution.py:62
  206.3 3.3 %gather_fusion.4 = bf16[4,8,48,256]{2,1,3,0:T(8,128)(2,1)} fusion(bf16[8,48,288]{1,0,2:T(8,128)(2,1)} %pad.63.clone, s32[4]{0:T(128)S(1)} %shift-left_bitcast_fusion), kind=kCustom, calls=%fused_computation.4 | custom fusion | bytes 1572912 | tf_op jit(solution)/shard_map/vmap()/gather | solution.py:62
  209.6 3.3 %gather_fusion.6 = bf16[4,8,48,256]{2,1,3,0:T(8,128)(2,1)} fusion(bf16[8,48,288]{1,0,2:T(8,128)(2,1)} %pad.65.clone, s32[4]{0:T(128)S(1)} %shift-left_bitcast_fusion), kind=kCustom, calls=%fused_computation.6 | custom fusion | bytes 1572912 | tf_op jit(solution)/shard_map/vmap()/gather | solution.py:62
  212.8 3.2 %gather_fusion.7 = bf16[4,8,48,256]{2,1,3,0:T(8,128)(2,1)} fusion(bf16[8,48,288]{1,0,2:T(8,128)(2,1)} %pad.66.clone, s32[4]{0:T(128)S(1)} %shift-left_bitcast_fusion), kind=kCustom, calls=%fused_computation.7 | custom fusion | bytes 1572912 | tf_op jit(solution)/shard_map/vmap()/gather | solution.py:62
  216.0 2.7 fusion.137
  218.8 2.2 copy.185
  222.9 2.2 copy.184
  235.3 2.3 copy.167
  237.7 2.3 copy.169
  240.0 2.3 copy.165
  243.7 3.2 %gather_fusion.1 = bf16[4,8,48,256]{2,1,3,0:T(8,128)(2,1)} fusion(bf16[8,48,288]{1,0,2:T(8,128)(2,1)} %pad.60.clone, s32[4]{0:T(128)S(1)} %shift-left_bitcast_fusion), kind=kCustom, calls=%fused_computation.1 | custom fusion | bytes 1572912 | tf_op jit(solution)/shard_map/vmap()/gather | solution.py:62
  246.9 3.2 %gather_fusion = bf16[4,8,48,256]{2,1,3,0:T(8,128)(2,1)} fusion(bf16[8,48,288]{1,0,2:T(8,128)(2,1)} %pad.59.clone, s32[4]{0:T(128)S(1)} %shift-left_bitcast_fusion), kind=kCustom, calls=%fused_computation | custom fusion | bytes 1572912 | tf_op jit(solution)/shard_map/vmap()/gather | solution.py:62
  250.1 3.2 %gather_fusion.2 = bf16[4,8,48,256]{2,1,3,0:T(8,128)(2,1)} fusion(bf16[8,48,288]{1,0,2:T(8,128)(2,1)} %pad.61.clone, s32[4]{0:T(128)S(1)} %shift-left_bitcast_fusion), kind=kCustom, calls=%fused_computation.2 | custom fusion | bytes 1572912 | tf_op jit(solution)/shard_map/vmap()/gather | solution.py:62
  253.4 3.2 %gather_fusion.3 = bf16[4,8,48,256]{2,1,3,0:T(8,128)(2,1)} fusion(bf16[8,48,288]{1,0,2:T(8,128)(2,1)} %pad.62.clone, s32[4]{0:T(128)S(1)} %shift-left_bitcast_fusion), kind=kCustom, calls=%fused_computation.3 | custom fusion | bytes 1572912 | tf_op jit(solution)/shard_map/vmap()/gather | solution.py:62
  256.5 11.0 %multiply_add_fusion = f32[4,8,48,256]{2,1,3,0:T(8,128)} fusion(bf16[4,8,48,256]{2,1,3,0:T(8,128)(2,1)} %gather_fusion.7, bf16[4,8,48,256]{2,1,3,0:T(8,128)(2,1)} %gather_fusion.6, bf16[4,8,48,256]{2,1,3,0:T(8,128)(2,1)} %gather_fusion.5, bf16[4,8,48,256]{2,1,3,0:T(8,128)(2,1)} %gather_fusion.4, bf16[4,8,48,256]{2,1,3,0:T(8,128)(2,1)} %gather_fusion.3, ...), kind=kLoop, calls=%fused_computation.8 | loop fusion | flops 9043968 | bytes 11010048 | tf_op jit(solution)/shard_map/add | solution.py:64
  267.5 3.7 %copy.179 = f32[4,8,48,256]{3,2,1,0:T(8,128)} copy(f32[4,8,48,256]{2,1,3,0:T(8,128)} %multiply_add_fusion) | data formatting | bytes 3145728 | tf_op jit(solution)/shard_map/add | solution.py:64
  (94 shorter events, 53.8 us)
Async XLA Ops:
  6.5 185.2 %all-reduce.16.cloned.1.call-start = ((), (), s32[]{:S(2)}) async-start(), calls=%async_computation | async-start | bytes 6291456 | tf_op jit(solution)/shard_map/psum | solution.py:24
  8.1 4.8 %copy-start.5 = (f32[1,1,2,8,48,256]{5,4,3,2,1,0:T(8,128)}, f32[1,1,2,8,48,256]{5,4,3,2,1,0:T(8,128)S(1)}, u32[]{:S(2)}) copy-start(f32[1,1,2,8,48,256]{5,4,3,2,1,0:T(8,128)S(1)} %get-tuple-element.58) | copy-start | bytes 2359300
  8.1 4.5 %copy-start.7 = (f32[8,48,256]{2,1,0:T(8,128)S(1)}, f32[8,48,256]{2,1,0:T(8,128)}, u32[]{:S(2)}) copy-start(f32[8,48,256]{2,1,0:T(8,128)} %param.15) | copy-start | bytes 1179652
  8.8 4.1 %collective-permute-start.1 = (f32[1,2,4,48,256]{4,3,2,1,0:T(8,128)S(1)}, f32[1,2,4,48,256]{4,3,2,1,0:T(8,128)S(1)}, u32[]{:S(2)}, u32[]{:S(2)}) collective-permute-start(f32[1,2,4,48,256]{4,3,2,1,0:T(8,128)S(1)} %copy.141), channel_id=1, source_target_pairs={{0,1},{2,3},{4,5},{6,7},{8,9},{10,11},{12,13},{14,15},{16,17},{18,... | collective-permute-start | bytes 1179656 | tf_op jit(solution)/shard_map/ppermute | solution.py:16
  11.3 3.6 %collective-permute-start = (f32[1,2,4,48,256]{4,3,2,1,0:T(8,128)S(1)}, f32[1,2,4,48,256]{4,3,2,1,0:T(8,128)S(1)}, u32[]{:S(2)}, u32[]{:S(2)}) collective-permute-start(f32[1,2,4,48,256]{4,3,2,1,0:T(8,128)S(1)} %copy.139), channel_id=1, source_target_pairs={{1,0},{3,2},{5,4},{7,6},{9,8},{11,10},{13,12},{15,14},{17,16},{19,... | collective-permute-start | bytes 1179656 | tf_op jit(solution)/shard_map/ppermute | solution.py:17
  12.8 3.8 %copy-start.2 = (f32[8,48,256]{2,0,1:T(8,128)}, f32[8,48,256]{2,0,1:T(8,128)S(1)}, u32[]{:S(2)}) copy-start(f32[8,48,256]{2,0,1:T(8,128)S(1)} %copy.138) | copy-start | bytes 1179652
  21.2 3.5 %collective-permute-start.3 = (f32[1,2,4,48,256]{4,3,2,1,0:T(8,128)S(1)}, f32[1,2,4,48,256]{4,3,2,1,0:T(8,128)S(1)}, u32[]{:S(2)}, u32[]{:S(2)}) collective-permute-start(f32[1,2,4,48,256]{4,3,2,1,0:T(8,128)S(1)} %copy.147), channel_id=1, source_target_pairs={{0,1},{2,3},{4,5},{6,7},{8,9},{10,11},{12,13},{14,15},{16,17},{18,... | collective-permute-start | bytes 1179656 | tf_op jit(solution)/shard_map/ppermute | solution.py:16
  23.3 3.6 %collective-permute-start.2 = (f32[1,2,4,48,256]{4,3,2,1,0:T(8,128)S(1)}, f32[1,2,4,48,256]{4,3,2,1,0:T(8,128)S(1)}, u32[]{:S(2)}, u32[]{:S(2)}) collective-permute-start(f32[1,2,4,48,256]{4,3,2,1,0:T(8,128)S(1)} %copy.145), channel_id=1, source_target_pairs={{1,0},{3,2},{5,4},{7,6},{9,8},{11,10},{13,12},{15,14},{17,16},{19,... | collective-permute-start | bytes 1179656 | tf_op jit(solution)/shard_map/ppermute | solution.py:17
  24.9 3.8 %copy-start.3 = (f32[8,48,256]{2,0,1:T(8,128)S(1)}, f32[8,48,256]{2,0,1:T(8,128)}, u32[]{:S(2)}) copy-start(f32[8,48,256]{2,0,1:T(8,128)} %copy-done.2) | copy-start | bytes 1179652
  24.9 3.8 %copy-start.6 = (f32[1,1,2,8,48,256]{5,4,3,2,1,0:T(8,128)S(1)}, f32[1,1,2,8,48,256]{5,4,3,2,1,0:T(8,128)}, u32[]{:S(2)}) copy-start(f32[1,1,2,8,48,256]{5,4,3,2,1,0:T(8,128)} %copy-done.5) | copy-start | bytes 2359300
  28.7 3.7 %copy-start.8 = (f32[1,4,8,256]{3,2,1,0:T(8,128)S(1)}, f32[1,4,8,256]{3,2,1,0:T(8,128)}, u32[]{:S(2)}) copy-start(f32[1,4,8,256]{3,2,1,0:T(8,128)} %param.14) | copy-start | bytes 98308
  32.6 3.6 %collective-permute-start.5 = (f32[1,2,4,48,256]{4,3,2,1,0:T(8,128)S(1)}, f32[1,2,4,48,256]{4,3,2,1,0:T(8,128)S(1)}, u32[]{:S(2)}, u32[]{:S(2)}) collective-permute-start(f32[1,2,4,48,256]{4,3,2,1,0:T(8,128)S(1)} %copy.153), channel_id=1, source_target_pairs={{0,1},{2,3},{4,5},{6,7},{8,9},{10,11},{12,13},{14,15},{16,17},{18,... | collective-permute-start | bytes 1179656 | tf_op jit(solution)/shard_map/ppermute | solution.py:16
  34.7 3.6 %collective-permute-start.4 = (f32[1,2,4,48,256]{4,3,2,1,0:T(8,128)S(1)}, f32[1,2,4,48,256]{4,3,2,1,0:T(8,128)S(1)}, u32[]{:S(2)}, u32[]{:S(2)}) collective-permute-start(f32[1,2,4,48,256]{4,3,2,1,0:T(8,128)S(1)} %copy.151), channel_id=1, source_target_pairs={{1,0},{3,2},{5,4},{7,6},{9,8},{11,10},{13,12},{15,14},{17,16},{19,... | collective-permute-start | bytes 1179656 | tf_op jit(solution)/shard_map/ppermute | solution.py:17
  43.5 4.7 %copy-start.9 = (s32[4]{0:T(128)S(1)}, s32[4]{0:T(128)}, u32[]{:S(2)}) copy-start(s32[4]{0:T(128)} %param.16) | copy-start | bytes 52
  43.5 0.9 copy-start
  44.5 7.5 %copy-start.1 = (f32[1,2,8,48,256]{4,2,3,1,0:T(8,128)S(1)}, f32[1,2,8,48,256]{4,2,3,1,0:T(8,128)}, u32[]{:S(2)}) copy-start(f32[1,2,8,48,256]{4,2,3,1,0:T(8,128)} %copy-done) | copy-start | bytes 2359300
  44.6 6.9 %collective-permute-start.7 = (f32[1,2,4,48,256]{4,3,2,1,0:T(8,128)S(1)}, f32[1,2,4,48,256]{4,3,2,1,0:T(8,128)S(1)}, u32[]{:S(2)}, u32[]{:S(2)}) collective-permute-start(f32[1,2,4,48,256]{4,3,2,1,0:T(8,128)S(1)} %copy.159), channel_id=1, source_target_pairs={{0,1},{2,3},{4,5},{6,7},{8,9},{10,11},{12,13},{14,15},{16,17},{18,... | collective-permute-start | bytes 1179656 | tf_op jit(solution)/shard_map/ppermute | solution.py:16
  46.9 4.9 %collective-permute-start.6 = (f32[1,2,4,48,256]{4,3,2,1,0:T(8,128)S(1)}, f32[1,2,4,48,256]{4,3,2,1,0:T(8,128)S(1)}, u32[]{:S(2)}, u32[]{:S(2)}) collective-permute-start(f32[1,2,4,48,256]{4,3,2,1,0:T(8,128)S(1)} %copy.157), channel_id=1, source_target_pairs={{1,0},{3,2},{5,4},{7,6},{9,8},{11,10},{13,12},{15,14},{17,16},{19,... | collective-permute-start | bytes 1179656 | tf_op jit(solution)/shard_map/ppermute | solution.py:17
  51.8 1.7 copy-start.4
  58.0 1.8 copy-start.10
Sparse Core Ops, SparseCore 0:
  60.0 131.7 all-reduce.15
where the time goes:
time: 279 us; the launch traced here: 278 us
  waiting for transfers between devices  138 us (49%)
  local copies, waits for them, and re-layouts  70.3 us (25%)
  other arithmetic  39.5 us (14%)
  between operations  16.6 us (6%)
  starting transfers between devices  14.1 us (5%)
    psum x1, waiting for transfers between devices, spread(): return lax.psum(kept, axis)  132 us
    gather x8, local copies, waits for them, and re-layouts, correlate(): lax.dynamic_slice_in_dim(padded, half_span + lag_value, cells_x, 2)  25.8 us
    add x4, other arithmetic, propagate_step(): advanced = 2.0 * current - earlier + courant_sq * laplace(extended)  14.4 us
    convert_element_type x8, local copies, waits for them, and re-layouts, correlate(): source.astype(jnp.float32)[None] * moved.astype(jnp.float32)  12.1 us
    unnamed x33, local copies, waits for them, and re-layouts  11.8 us
    pad x8, local copies, waits for them, and re-layouts, correlate(): padded = jnp.pad(receiver, ((0, 0), (0, 0), (half_span, half_span)))  11.6 us
    add x1, other arithmetic, correlate(): image_acc + source.astype(jnp.float32)[None] * moved.astype(jnp.float32)  11 us
    ppermute x4, starting transfers between devices, extended_2(): before = lax.ppermute(last, axis, up)  8.75 us
  transfers between devices with their start and end apart: 9, of which 4 were waited for; matrix products, arithmetic and copies ran while one was open for 1% of the time, Pallas kernels for 0%

commit v1 on v0

--- a/solution.py
+++ b/solution.py
@@ -1,9 +1,19 @@
+import functools
 import jax
 import jax.numpy as jnp
 from jax import lax
+from jax.experimental import pallas as pl
+from jax.experimental.pallas import tpu as pltpu
 from jax.sharding import PartitionSpec as P
 
 stencil_taps = (-205.0 / 72.0, 8.0 / 5.0, -1.0 / 5.0, 8.0 / 315.0, -1.0 / 560.0)
+REACH = 4
+COMMON, BAND_UNIT = 5040.0, 4096.0
+TAPS = tuple(round(tap * COMMON) / BAND_UNIT for tap in stencil_taps)
+LANES = 128
+SUBLANES = 8
+VMEM = pl.BlockSpec(memory_space=pltpu.VMEM)
+SMEM = pl.BlockSpec(memory_space=pltpu.SMEM)
 
 
 def extended_2(shard, sides, width):
@@ -64,7 +74,7 @@
     return image_acc + source.astype(jnp.float32)[None] * moved.astype(jnp.float32)
 
 
-def on_device(checkpoint, traces, courant_sq, holder, offset_lags):
+def on_device_general(checkpoint, traces, courant_sq, holder, offset_lags):
     shot_count = holder.shape[0]
     step_count = traces.shape[1]
     my_lags = offset_lags[0]
@@ -88,6 +98,360 @@
     return image_acc
 
 
+def half_kernel(spec, *refs):
+    step_no, near, last = spec
+    refs = list(refs)
+    side = refs.pop(0)[0]
+    if last and near:
+        me_ref, lags_ref = refs.pop(0), refs.pop(0)
+    courant_ref, drive_ref, band_ref = refs.pop(0), refs.pop(0), refs.pop(0)
+    start_ref = refs.pop(0) if step_no < 2 else None
+    before_ref = refs.pop(0) if step_no >= 2 else None
+    current_ref = refs.pop(0) if step_no >= 1 else None
+    halo_ref = refs.pop(0) if near else None
+    fresh_ref = refs.pop(0) if near else None
+    along_x, split, ext = refs.pop(), refs.pop(), refs.pop()
+    out_ref = refs.pop(0)
+    fields, planes, cells_z, cells_x = out_ref.shape
+    count = planes // 2
+    tiles_x = cells_x // LANES
+    everything = slice(None)
+
+    def row_y(d):
+        return jnp.where(side == 0, planes - 1 - d, d)
+
+    def current(f, d, at=()):
+        if d < 0:
+            j = -1 - d
+            if step_no == 0:
+                j = jnp.where(side == 0, j, REACH - 1 - j)
+            return halo_ref[(f, j, *at)]
+        if step_no == 0:
+            return start_ref[(1, f, row_y(d), *at)]
+        return current_ref[(f, d, *at)]
+
+    def before(f, d, at=()):
+        if step_no < 2:
+            return start_ref[(step_no, f, row_y(d), *at)]
+        return before_ref[(f, d, *at)]
+
+    base = 0 if near else count
+    pad = jnp.zeros((SUBLANES, LANES), jnp.float32)
+    for f in range(fields):
+        for i in range(count):
+            here = current(f, base + i)
+            for t in range(tiles_x):
+                ext[f, i, t, pl.ds(0, SUBLANES)] = pad
+                ext[f, i, t, pl.ds(SUBLANES, cells_z)] = here[:, t * LANES : (t + 1) * LANES]
+                ext[f, i, t, pl.ds(SUBLANES + cells_z, SUBLANES)] = pad
+            high = here.astype(jnp.bfloat16)
+            left = here - high.astype(jnp.float32)
+            middle = left.astype(jnp.bfloat16)
+            low = (left - middle.astype(jnp.float32)).astype(jnp.bfloat16)
+            at = pl.ds((f * count + i) * cells_z, cells_z)
+            for j, piece in enumerate((high, middle, low)):
+                split[at, pl.ds(j * cells_x, cells_x)] = piece
+    band = band_ref[...]
+    along_x[...] = jnp.dot(
+        split[...], jnp.concatenate([band] * 3, axis=0), preferred_element_type=jnp.float32
+    )
+    for i in range(count):
+        d = base + i
+        y = row_y(d)
+        for t in range(tiles_x):
+            across = pl.ds(t * LANES, LANES)
+            at = (everything, across)
+            courant = courant_ref[y, :, across] * (BAND_UNIT / COMMON)
+            for f in range(fields):
+                here = ext[f, i, t, pl.ds(SUBLANES, cells_z)]
+                lap = (3.0 * TAPS[0]) * here
+                lap += along_x[pl.ds((f * count + i) * cells_z, cells_z), across]
+                for tap in range(1, REACH + 1):
+                    beside = (
+                        ext[f, i, t, pl.ds(SUBLANES + tap, cells_z)]
+                        + ext[f, i, t, pl.ds(SUBLANES - tap, cells_z)]
+                    )
+                    for other in (d - tap, d + tap):
+                        if other < planes:
+                            beside += current(f, other, at)
+                    lap += TAPS[tap] * beside
+                out_ref[f, d, :, across] = (2.0 * here - before(f, d, at)) + courant * lap
+        out_ref[1, d, pl.ds(0, 1)] = (
+            out_ref[1, d, pl.ds(0, 1)] + drive_ref[step_no, pl.ds(y, 1)]
+        )
+    if not near:
+        return
+    for f in range(fields):
+        for d in range(count, planes):
+            out_ref[f, d] = fresh_ref[f, d]
+    if not last:
+        edge_ref = refs.pop(0)
+        for f in range(fields):
+            for d in range(REACH):
+                edge_ref[f, d] = out_ref[f, d]
+        return
+    me = me_ref[0]
+    row = lax.broadcasted_iota(jnp.int32, (SUBLANES, cells_x), 0)
+    tail = jnp.zeros((SUBLANES, cells_x), jnp.float32)
+    for i in range(lags_ref.shape[1]):
+        tail = jnp.where(row == i, lags_ref[0, i].astype(jnp.float32), tail)
+    for k, part_ref in enumerate(refs):
+        d = row_y(jnp.bitwise_xor(me, k))
+        for f in range(fields):
+            part_ref[pl.ds(f * cells_z, cells_z)] = before_ref[f, d].astype(jnp.bfloat16)
+            part_ref[pl.ds((fields + f) * cells_z, cells_z)] = out_ref[f, d].astype(jnp.bfloat16)
+        part_ref[pl.ds(2 * fields * cells_z, SUBLANES)] = tail.astype(jnp.bfloat16)
+
+
+def half_step(spec, side, extra, constant, levels, halo, groups):
+    _, near, last = spec
+    fields, planes, cells_z, cells_x = levels[0].shape[-4:]
+    shape = jax.ShapeDtypeStruct
+    full = shape((fields, planes, cells_z, cells_x), jnp.float32)
+    outs, scratch = [full], []
+    if near and last:
+        rows = 2 * fields * cells_z + SUBLANES
+        outs = [shape((rows, cells_x), jnp.bfloat16)] * groups
+        scratch = [pltpu.VMEM(full.shape, full.dtype)]
+    elif near:
+        outs += [shape((fields, REACH, cells_z, cells_x), jnp.float32)]
+    count = planes // 2
+    cells = fields * count * cells_z * cells_x
+    args = [side, *extra, *constant, *levels, *halo]
+    scalars = 1 + len(extra)
+
+    def kernel(*refs):
+        if near and last:
+            ins, refs = refs[: len(args)], refs[len(args) :]
+            refs = (*ins, refs[groups], *refs[:groups], *refs[groups + 1 :])
+        half_kernel(spec, *refs)
+
+    return pl.pallas_call(
+        kernel,
+        out_shape=outs,
+        in_specs=[SMEM] * scalars + [VMEM] * (len(args) - scalars),
+        out_specs=[VMEM] * len(outs),
+        scratch_shapes=[
+            *scratch,
+            pltpu.VMEM(
+                (fields, count, cells_x // LANES, cells_z + 2 * SUBLANES, LANES), jnp.float32
+            ),
+            pltpu.VMEM((fields * count * cells_z, 3 * cells_x), jnp.bfloat16),
+            pltpu.VMEM((fields * count * cells_z, cells_x), jnp.float32),
+        ],
+        compiler_params=pltpu.CompilerParams(vmem_limit_bytes=8 * 1024 * 1024),
+        cost_estimate=pl.CostEstimate(
+            flops=2000 * cells, bytes_accessed=16 * cells, transcendentals=0
+        ),
+        name="near" if near else "far",
+    )(*args)
+
+
+def turned_x(tiles, step, lane):
+    count = len(tiles)
+    if step == 0:
+        return tiles
+    if step > 0:
+        rolled = [pltpu.roll(t, LANES - step, 1) for t in tiles]
+        keep = lane < LANES - step
+        return [jnp.where(keep, rolled[i], rolled[(i + 1) % count]) for i in range(count)]
+    rolled = [pltpu.roll(t, -step, 1) for t in tiles]
+    keep = lane >= -step
+    return [jnp.where(keep, rolled[i], rolled[i - 1]) for i in range(count)]
+
+
+FINE = 4
+
+
+def image_kernel(spec, valid_ref, *refs):
+    ours, groups, snaps, fields, start, finish = spec
+    refs = list(refs)
+    parts = [refs.pop(0) for _ in ours]
+    before = None if start else refs.pop(0)
+    tails = [refs.pop(0) for _ in range(groups)] if finish else []
+    held, coarse, fine = refs[-3:]
+    refs = refs[:-3]
+    image = refs.pop() if finish else refs.pop(0)
+    outs = refs
+    offsets, cells_z, cells_x = image.shape
+    half = offsets // 2
+    tail = snaps * fields * cells_z
+    place = 0
+    for k, part in zip(ours, parts):
+
+        @pl.when(valid_ref[k] > 0)
+        def _(part=part, place=place):
+            for i in range(snaps * fields):
+                held[place, i] = part[pl.ds(i * cells_z, cells_z)].astype(jnp.float32)
+
+        place = place + valid_ref[k]
+    tiles_x = cells_x // LANES
+    rows = 2 * SUBLANES
+    lane = lax.broadcasted_iota(jnp.int32, (rows, LANES), 1)
+    join = lambda tiles: jnp.concatenate(tiles, axis=1)
+    cut = lambda value: [value[:, t * LANES : (t + 1) * LANES] for t in range(tiles_x)]
+
+    for h in range(offsets):
+        image[h] = jnp.zeros((cells_z, cells_x), jnp.float32) if start else before[h]
+
+    def one(j, carry):
+        shot, z = j // (cells_z // rows), lax.rem(j, cells_z // rows)
+        at = pl.ds(pl.multiple_of(z * rows, rows), rows)
+        for m in range(snaps):
+            receiver = cut(held[shot, m * fields + 1, at])
+            for b in range(offsets // FINE):
+                coarse[m, b] = join(turned_x(receiver, FINE * b - half, lane))
+            source = cut(held[shot, m * fields, at])
+            for a in range(FINE):
+                fine[m, a] = join(turned_x(source, -a, lane))
+        for a in range(FINE):
+            for b in range(offsets // FINE):
+                total = image[FINE * b + a, at]
+                for m in range(snaps):
+                    total += fine[m, a] * coarse[m, b]
+                image[FINE * b + a, at] = total
+        return carry
+
+    lax.fori_loop(0, place * (cells_z // rows), one, 0)
+    if not finish:
+        return
+    lane = lax.broadcasted_iota(jnp.int32, (cells_z, LANES), 1)
+    for k, out in enumerate(outs):
+        ends = tails[k][pl.ds(tail, SUBLANES)].astype(jnp.float32)
+        for i in range(out.shape[0]):
+            lag = ends[i, 0].astype(jnp.int32)
+            place = half + lag
+            back = lax.rem(place, FINE)
+            tiles = [image[place, :, pl.ds(t * LANES, LANES)] for t in range(tiles_x)]
+            rolled = [pltpu.roll(tile, lax.rem(LANES - back, LANES), 1) for tile in tiles]
+            keep = lane < LANES - back
+            for t in range(tiles_x):
+                x = lane + (t * LANES + lag)
+                value = jnp.where(keep, rolled[t], rolled[(t + 1) % tiles_x])
+                value = jnp.where((x >= 0) & (x < cells_x), value, 0.0)
+                out[i, :, pl.ds(t * LANES, LANES)] = value.astype(out.dtype)
+
+
+def imaged(spec, valid, parts, before, offsets):
+    ours, groups, snaps, fields, start, finish = spec
+    rows, cells_x = parts[0].shape
+    cells_z = (rows - SUBLANES) // (snaps * fields)
+    shape = jax.ShapeDtypeStruct
+    if finish:
+        per_group = offsets // groups
+        outs = [shape((per_group, cells_z, cells_x), jnp.bfloat16)] * groups
+        outs[0] = shape((per_group, cells_z, cells_x), jnp.float32)
+    else:
+        outs = [shape((offsets, cells_z, cells_x), jnp.float32)]
+    args = [valid, *[parts[k] for k in ours]]
+    args += [] if start else [before]
+    args += [parts[k] for k in range(groups)] if finish else []
+    scratch = [pltpu.VMEM((offsets, cells_z, cells_x), jnp.float32)] if finish else []
+    strip = (2 * SUBLANES, cells_x)
+    made = pl.pallas_call(
+        functools.partial(image_kernel, spec),
+        out_shape=outs,
+        in_specs=[SMEM] + [VMEM] * (len(args) - 1),
+        out_specs=[VMEM] * len(outs),
+        scratch_shapes=[
+            *scratch,
+            pltpu.VMEM((len(ours), snaps * fields, cells_z, cells_x), jnp.float32),
+            pltpu.VMEM((snaps, offsets // FINE, *strip), jnp.float32),
+            pltpu.VMEM((snaps, FINE, *strip), jnp.float32),
+        ],
+        compiler_params=pltpu.CompilerParams(vmem_limit_bytes=8 * 1024 * 1024),
+        cost_estimate=pl.CostEstimate(
+            flops=200 * snaps * len(ours) * offsets * cells_z * cells_x,
+            bytes_accessed=8 * offsets * cells_z * cells_x,
+            transcendentals=0,
+        ),
+        name="image",
+    )(*args)
+    return made if finish else made[0]
+
+
+def gather_kernel(me_ref, *refs):
+    out_ref = refs[-1]
+    for k, part_ref in enumerate(refs[:-1]):
+        y = jnp.bitwise_xor(me_ref[0], k)
+        for i in range(out_ref.shape[0]):
+            out_ref[i, y] = part_ref[i].astype(jnp.float32)
+
+
+def far_first(groups):
+    order = (4, 5, 7, 3, 6, 2, 1)
+    return [k for k in order if k < groups] + [k for k in range(8, groups)]
+
+
+def on_device_planes(checkpoint, traces, courant_sq, holder, offset_lags):
+    start = checkpoint[0]
+    fields, planes, cells_z, cells_x = start.shape[1:]
+    step_count = traces.shape[1]
+    groups = lax.axis_size("off")
+    per_group = offset_lags.shape[1]
+    snaps = step_count // 2
+    me = lax.axis_index("off").astype(jnp.int32)
+    side = lax.axis_index("gy").astype(jnp.int32)
+    slots = jnp.bitwise_xor(me, jnp.arange(groups, dtype=jnp.int32))
+    valid = jnp.any(holder[None, :] == slots[:, None], axis=1).astype(jnp.int32)
+    side1, me1 = side.reshape(1), me.reshape(1)
+    swap = [(0, 1), (1, 0)]
+
+    apart = jnp.abs(
+        lax.broadcasted_iota(jnp.int32, (cells_x, cells_x), 0)
+        - lax.broadcasted_iota(jnp.int32, (cells_x, cells_x), 1)
+    )
+    band = jnp.zeros((cells_x, cells_x), jnp.float32)
+    for tap in range(1, REACH + 1):
+        band = jnp.where(apart == tap, TAPS[tap], band)
+    band = band.astype(jnp.bfloat16)
+
+    edge = lax.dynamic_slice(
+        checkpoint,
+        (0, 1, 0, (1 - side) * (planes - REACH), 0, 0),
+        (1, 1, fields, REACH, cells_z, cells_x),
+    )[0, 0]
+    earlier = current = None
+    constant = [courant_sq, traces[0], band]
+    for n in range(step_count):
+        halo = lax.ppermute(edge, "gy", swap)
+        last = n == step_count - 1
+        levels = [start] if n == 0 else [start, current] if n == 1 else [earlier, current]
+        fresh = half_step((n, False, last), side1, [], constant, levels, [], groups)[0]
+        extra = [me1, offset_lags] if last else []
+        made = half_step(
+            (n, True, last), side1, extra, constant, levels, [halo, fresh], groups
+        )
+        if not last:
+            earlier, (current, edge) = current, made
+    parts = made
+
+    def pairs(k):
+        return [(i, i ^ k) for i in range(groups)]
+
+    order = far_first(groups)
+    got, back = {0: parts[0]}, {}
+    for k in order:
+        got[k] = lax.ppermute(parts[k], "off", pairs(k))
+    offsets = groups * per_group
+    stages = ((0, 4, 7, 6), (5, 3, 2, 1))
+    images = None
+    for i, ours in enumerate(stages):
+        spec = (ours, groups, snaps, fields, i == 0, i == len(stages) - 1)
+        images = imaged(spec, valid, got, images, offsets)
+    for k in order:
+        back[k] = lax.ppermute(images[k], "off", pairs(k))
+    back[0] = images[0]
+    return pl.pallas_call(
+        gather_kernel,
+        out_shape=jax.ShapeDtypeStruct((per_group, planes, cells_z, cells_x), jnp.float32),
+        in_specs=[SMEM] + [VMEM] * groups,
+        out_specs=VMEM,
+        compiler_params=pltpu.CompilerParams(vmem_limit_bytes=8 * 1024 * 1024),
+        name="gather",
+    )(me1, *[back[k] for k in range(groups)])
+
+
 def solution(mesh):
     placed = (
         P(("survey", "off"), None, None, "gy", None, None),
@@ -96,6 +460,25 @@
         P("survey"),
         P(("survey", "off"), None),
     )
+
+    def on_device(checkpoint, traces, courant_sq, holder, offset_lags):
+        groups, sides = mesh.shape["off"], mesh.shape["gy"]
+        planes, cells_z, cells_x = courant_sq.shape
+        fits = (
+            groups == planes
+            and groups & (groups - 1) == 0
+            and sides == 2
+            and planes == 2 * REACH
+            and cells_z % (2 * SUBLANES) == 0
+            and cells_x % LANES == 0
+            and cells_x >= 2 * LANES
+            and traces.shape[1] == 4
+            and groups * offset_lags.shape[1] <= LANES
+            and offset_lags.shape[1] <= SUBLANES
+        )
+        chosen = on_device_planes if fits else on_device_general
+        return chosen(checkpoint, traces, courant_sq, holder, offset_lags)
+
     return jax.shard_map(
         on_device,
         mesh=mesh,

time: 279 us -> 64.7 us (0.23)
  waiting for transfers between devices: 138 us -> 16.2 us
  local copies, waits for them, and re-layouts: 70.3 us -> 4.2 us
  other arithmetic: 39.5 us -> 0.16 us
  starting transfers between devices: 14.1 us -> 31 us
  between operations: 16.6 us -> 0.14 us
  Pallas kernels: 0 us -> 12.1 us
    psum x1 -> x0, waiting for transfers between devices: 132 us -> none  [spread(): return lax.psum(kept, axis)]
    gather x8 -> x0, local copies, waits for them, and re-layouts: 25.8 us -> none  [correlate(): lax.dynamic_slice_in_dim(padded, half_span + lag_value, cells_x, 2)]
    add x5 -> x0, other arithmetic: 25.3 us -> none  [the longest x4 14.4 us: propagate_step(): advanced = 2.0 * current - earlier + courant_sq * laplace(extended)]
    ppermute x8 -> x18, starting transfers between devices: 14.1 us -> 31 us  [the longest x7 18.8 us: on_device_planes(): got[k] = lax.ppermute(parts[k], 'off', pairs(k))]
    pallas_call x0 -> x11, Pallas kernels: none -> 12.1 us  [the longest x8 6.66 us: half_step(): pl.pallas_call(kernel, out_shape=outs, in_specs=[SMEM] * scalars + [VMEM]...]
    convert_element_type x8 -> x0, local copies, waits for them, and re-layouts: 12.1 us -> none  [correlate(): source.astype(jnp.float32)[None] * moved.astype(jnp.float32)]
    pad x8 -> x0, local copies, waits for them, and re-layouts: 11.6 us -> none  [correlate(): padded = jnp.pad(receiver, ((0, 0), (0, 0), (half_span, half_span)))]
    ppermute x8 -> x18, waiting for transfers between devices: 5.67 us -> 16.2 us  [the longest x7 9.35 us: on_device_planes(): back[k] = lax.ppermute(images[k], 'off', pairs(k))]
  transfers between devices with their start and end apart: 9 -> 18, of which waited for: 4 -> 8; matrix products, arithmetic and copies ran while one was open for 1% -> 0% of each run, Pallas kernels for 0% -> 7%
where the time goes in v1:
time: 64.7 us; the launch traced here: 63.8 us
  starting transfers between devices  31 us (48%)
  waiting for transfers between devices  16.2 us (25%)
  Pallas kernels  12.1 us (19%)
  local copies, waits for them, and re-layouts  4.2 us (6%)
    ppermute x7, starting transfers between devices, on_device_planes(): got[k] = lax.ppermute(parts[k], 'off', pairs(k))  18.8 us
    ppermute x7, starting transfers between devices, on_device_planes(): back[k] = lax.ppermute(images[k], 'off', pairs(k))  11.2 us
    ppermute x7, waiting for transfers between devices, on_device_planes(): back[k] = lax.ppermute(images[k], 'off', pairs(k))  9.35 us
    pallas_call x8, Pallas kernels, half_step(): pl.pallas_call(kernel, out_shape=outs, in_specs=[SMEM] * scalars + [VMEM]...  6.66 us
    pallas_call x2, Pallas kernels, imaged(): pl.pallas_call(functools.partial(image_kernel, spec), out_shape=outs, in_...  4.23 us
    ppermute x7, waiting for transfers between devices, on_device_planes(): got[k] = lax.ppermute(parts[k], 'off', pairs(k))  4.01 us
    unnamed x14, local copies, waits for them, and re-layouts  3.18 us
    ppermute x4, waiting for transfers between devices, on_device_planes(): halo = lax.ppermute(edge, 'gy', swap)  2.81 us
  transfers between devices with their start and end apart: 18, of which 8 were waited for; matrix products, arithmetic and copies ran while one was open for 0% of the time, Pallas kernels for 7%

profile of v1, /device:TPU:0, one launch (start us, length us, event | category | flops | bytes accessed | tf_op | source)
XLA Modules:
  0.0 63.8 jit_solution(6326483483795367347)
XLA Ops:
  0.0 1.0 %dynamic-slice_bitcast_fusion = f32[2,4,48,256]{3,2,1,0:T(8,128)S(1)} fusion(f32[1,2,2,8,48,256]{5,4,3,2,1,0:T(8,128)} %param.5, s32[]{:T(128)S(6)} %select_n.76), kind=kLoop, calls=%fused_computation | loop fusion | bytes 786436 | tf_op jit(solution)/shard_map/squeeze | solution.py:409
  1.7 1.4 %copy-done = f32[1,2,2,8,48,256]{5,4,3,2,1,0:T(8,128)S(1)} copy-done((f32[1,2,2,8,48,256]{5,4,3,2,1,0:T(8,128)S(1)}, f32[1,2,2,8,48,256]{5,4,3,2,1,0:T(8,128)}, u32[]{:S(2)}) %copy-start) | copy-done | bytes 1572888
  3.1 1.0 %copy-done.1 = f32[8,48,256]{2,1,0:T(8,128)S(1)} copy-done((f32[8,48,256]{2,1,0:T(8,128)S(1)}, f32[8,48,256]{2,1,0:T(8,128)}, u32[]{:S(2)}) %copy-start.1) | copy-done | bytes 393240
  12.6 1.0 %collective-permute-done.3.refs_8_ = f32[2,4,48,256]{3,2,1,0:T(8,128)S(1)} collective-permute-done((f32[2,4,48,256]{3,2,1,0:T(8,128)S(1)}, f32[2,4,48,256]{3,2,1,0:T(8,128)S(1)}, u32[]{:S(2)}, u32[]{:S(2)}) %collective-permute-start.3) | collective-permute-done | bytes 393248 | tf_op jit(solution)/shard_map/ppermute | solution.py:417
  13.5 1.3 %near.7 = (bf16[200,256]{1,0:T(8,128)(2,1)S(1)}, bf16[200,256]{1,0:T(8,128)(2,1)S(1)}, bf16[200,256]{1,0:T(8,128)(2,1)S(1)}, bf16[200,256]{1,0:T(8,128)(2,1)S(1)...) custom-call(s32[1]{0:T(128)} %bitcast.1.refs_0_, ...), custom_call_target="tpu_custom_call" | custom-call | flops 196608000 | bytes 1572864 | tf_op jit(solution)/shard_map/near/pallas_call | solution.py:229
  14.9 4.8 %collective-permute-start.10 = (bf16[200,256]{1,0:T(8,128)(2,1)S(1)}, bf16[200,256]{1,0:T(8,128)(2,1)S(1)}, u32[]{:S(2)}, u32[]{:S(2)}) collective-permute-start(bf16[200,256]{1,0:T(8,128)(2,1)S(1)} %get-tuple-element.40), channel_id=1, source_target_pairs={{0,12},{2,14},{4,8},{6,10},{8,4},{10,6},{12,0},{14,2},{1,13},{3,15... | collective-permute-start | bytes 307208 | tf_op jit(solution)/shard_map/ppermute | solution.py:435
  19.7 2.8 %collective-permute-start.9 = (bf16[200,256]{1,0:T(8,128)(2,1)S(1)}, bf16[200,256]{1,0:T(8,128)(2,1)S(1)}, u32[]{:S(2)}, u32[]{:S(2)}) collective-permute-start(bf16[200,256]{1,0:T(8,128)(2,1)S(1)} %get-tuple-element.39), channel_id=1, source_target_pairs={{0,14},{2,12},{4,10},{6,8},{8,6},{10,4},{12,2},{14,0},{1,15},{3,13... | collective-permute-start | bytes 307208 | tf_op jit(solution)/shard_map/ppermute | solution.py:435
  22.5 1.0 %collective-permute-start.4 = (bf16[200,256]{1,0:T(8,128)(2,1)S(1)}, bf16[200,256]{1,0:T(8,128)(2,1)S(1)}, u32[]{:S(2)}, u32[]{:S(2)}) collective-permute-start(bf16[200,256]{1,0:T(8,128)(2,1)S(1)} %get-tuple-element.33), channel_id=1, source_target_pairs={{0,10},{2,8},{4,14},{6,12},{8,2},{10,0},{12,6},{14,4},{1,11},{3,9}... | collective-permute-start | bytes 307208 | tf_op jit(solution)/shard_map/ppermute | solution.py:435
  23.5 2.4 %collective-permute-start.5 = (bf16[200,256]{1,0:T(8,128)(2,1)S(1)}, bf16[200,256]{1,0:T(8,128)(2,1)S(1)}, u32[]{:S(2)}, u32[]{:S(2)}) collective-permute-start(bf16[200,256]{1,0:T(8,128)(2,1)S(1)} %get-tuple-element.34), channel_id=1, source_target_pairs={{0,6},{2,4},{4,2},{6,0},{8,14},{10,12},{12,10},{14,8},{1,7},{3,5},... | collective-permute-start | bytes 307208 | tf_op jit(solution)/shard_map/ppermute | solution.py:435
  25.9 6.3 %collective-permute-start.6 = (bf16[200,256]{1,0:T(8,128)(2,1)S(1)}, bf16[200,256]{1,0:T(8,128)(2,1)S(1)}, u32[]{:S(2)}, u32[]{:S(2)}) collective-permute-start(bf16[200,256]{1,0:T(8,128)(2,1)S(1)} %get-tuple-element.35), channel_id=1, source_target_pairs={{0,4},{2,6},{4,0},{6,2},{8,12},{10,14},{12,8},{14,10},{1,5},{3,7},... | collective-permute-start | bytes 307208 | tf_op jit(solution)/shard_map/ppermute | solution.py:435
  32.2 1.6 %collective-permute-done.8.refs_1_.refs_9_ = bf16[200,256]{1,0:T(8,128)(2,1)S(1)} collective-permute-done((bf16[200,256]{1,0:T(8,128)(2,1)S(1)}, bf16[200,256]{1,0:T(8,128)(2,1)S(1)}, u32[]{:S(2)}, u32[]{:S(2)}) %collective-permute-start.8) | collective-permute-done | bytes 102432 | tf_op jit(solution)/shard_map/ppermute | solution.py:435
  33.8 1.5 %collective-permute-start.7 = (bf16[200,256]{1,0:T(8,128)(2,1)S(1)}, bf16[200,256]{1,0:T(8,128)(2,1)S(1)}, u32[]{:S(2)}, u32[]{:S(2)}) collective-permute-start(bf16[200,256]{1,0:T(8,128)(2,1)S(1)} %get-tuple-element.36), channel_id=1, source_target_pairs={{0,2},{2,0},{4,6},{6,4},{8,10},{10,8},{12,14},{14,12},{1,3},{3,1},... | collective-permute-start | bytes 307208 | tf_op jit(solution)/shard_map/ppermute | solution.py:435
  35.4 1.9 %image.2.refs_4_ = f32[32,48,256]{2,1,0:T(8,128)S(1)} custom-call(s32[8]{0:T(128)S(1)} %convert_element_type.20.valid_ref, bf16[200,256]{1,0:T(8,128)(2,1)S(1)} %get-tuple-element.37.refs_0_.refs_5_, bf16[200,256]{1,0:T(8,128)(2,1)S(1)} %collective-permute-done.8.refs_1_.refs_9_, bf16[200,256]{1,0:T(8,128)(2,1)S(1)} %collective-permute-done.9.refs_2_.refs_12_, ...), custom_call_target="tpu_custom_call" | custom-call | flops 629145600 | bytes 3145728 | tf_op jit(solution)/shard_map/image/pallas_call | solution.py:351
  37.3 1.3 %collective-permute-done.4.refs_0_.refs_10_ = bf16[200,256]{1,0:T(8,128)(2,1)S(1)} collective-permute-done((bf16[200,256]{1,0:T(8,128)(2,1)S(1)}, bf16[200,256]{1,0:T(8,128)(2,1)S(1)}, u32[]{:S(2)}, u32[]{:S(2)}) %collective-permute-start.4) | collective-permute-done | bytes 102432 | tf_op jit(solution)/shard_map/ppermute | solution.py:435
  38.6 1.1 %collective-permute-done.7.refs_3_.refs_6_ = bf16[200,256]{1,0:T(8,128)(2,1)S(1)} collective-permute-done((bf16[200,256]{1,0:T(8,128)(2,1)S(1)}, bf16[200,256]{1,0:T(8,128)(2,1)S(1)}, u32[]{:S(2)}, u32[]{:S(2)}) %collective-permute-start.7) | collective-permute-done | bytes 102432 | tf_op jit(solution)/shard_map/ppermute | solution.py:435
  39.7 2.3 %image.3 = (f32[4,48,256]{2,1,0:T(8,128)S(1)}, bf16[4,48,256]{2,1,0:T(8,128)(2,1)S(1)}, bf16[4,48,256]{2,1,0:T(8,128)(2,1)S(1)}, bf16[4,48,256]{2,1,0:T(8,128)(2...) custom-call(s32[8]{0:T(128)S(1)} %convert_element_type.20.valid_ref,, ...), custom_call_target="tpu_custom_call" | custom-call | flops 629145600 | bytes 3145728 | tf_op jit(solution)/shard_map/image/pallas_call | solution.py:351
  42.7 2.9 %collective-permute-start.13 = (bf16[4,48,256]{2,1,0:T(8,128)(2,1)S(1)}, bf16[4,48,256]{2,1,0:T(8,128)(2,1)S(1)}, u32[]{:S(2)}, u32[]{:S(2)}) collective-permute-start(bf16[4,48,256]{2,1,0:T(8,128)(2,1)S(1)} %get-tuple-element.44), channel_id=1, source_target_pairs={{0,6},{2,4},{4,2},{6,0},{8,14},{10,12},{12,10},{14,8},{1,7},{3,5},... | collective-permute-start | bytes 294920 | tf_op jit(solution)/shard_map/ppermute | solution.py:443
  45.6 1.1 %collective-permute-start.14 = (bf16[4,48,256]{2,1,0:T(8,128)(2,1)S(1)}, bf16[4,48,256]{2,1,0:T(8,128)(2,1)S(1)}, u32[]{:S(2)}, u32[]{:S(2)}) collective-permute-start(bf16[4,48,256]{2,1,0:T(8,128)(2,1)S(1)} %get-tuple-element.45), channel_id=1, source_target_pairs={{0,8},{2,10},{4,12},{6,14},{8,0},{10,2},{12,4},{14,6},{1,9},{3,11}... | collective-permute-start | bytes 294920 | tf_op jit(solution)/shard_map/ppermute | solution.py:443
  46.7 1.9 %collective-permute-start.15 = (bf16[4,48,256]{2,1,0:T(8,128)(2,1)S(1)}, bf16[4,48,256]{2,1,0:T(8,128)(2,1)S(1)}, u32[]{:S(2)}, u32[]{:S(2)}) collective-permute-start(bf16[4,48,256]{2,1,0:T(8,128)(2,1)S(1)} %get-tuple-element.46), channel_id=1, source_target_pairs={{0,10},{2,8},{4,14},{6,12},{8,2},{10,0},{12,6},{14,4},{1,11},{3,9}... | collective-permute-start | bytes 294920 | tf_op jit(solution)/shard_map/ppermute | solution.py:443
  48.5 2.6 %collective-permute-start.16 = (bf16[4,48,256]{2,1,0:T(8,128)(2,1)S(1)}, bf16[4,48,256]{2,1,0:T(8,128)(2,1)S(1)}, u32[]{:S(2)}, u32[]{:S(2)}) collective-permute-start(bf16[4,48,256]{2,1,0:T(8,128)(2,1)S(1)} %get-tuple-element.47), channel_id=1, source_target_pairs={{0,12},{2,14},{4,8},{6,10},{8,4},{10,6},{12,0},{14,2},{1,13},{3,15... | collective-permute-start | bytes 294920 | tf_op jit(solution)/shard_map/ppermute | solution.py:443
  51.1 2.1 %collective-permute-start.17 = (bf16[4,48,256]{2,1,0:T(8,128)(2,1)S(1)}, bf16[4,48,256]{2,1,0:T(8,128)(2,1)S(1)}, u32[]{:S(2)}, u32[]{:S(2)}) collective-permute-start(bf16[4,48,256]{2,1,0:T(8,128)(2,1)S(1)} %get-tuple-element.48), channel_id=1, source_target_pairs={{0,14},{2,12},{4,10},{6,8},{8,6},{10,4},{12,2},{14,0},{1,15},{3,13... | collective-permute-start | bytes 294920 | tf_op jit(solution)/shard_map/ppermute | solution.py:443
  53.2 6.4 %collective-permute-done.14.refs_4_ = bf16[4,48,256]{2,1,0:T(8,128)(2,1)S(1)} collective-permute-done((bf16[4,48,256]{2,1,0:T(8,128)(2,1)S(1)}, bf16[4,48,256]{2,1,0:T(8,128)(2,1)S(1)}, u32[]{:S(2)}, u32[]{:S(2)}) %collective-permute-start.14) | collective-permute-done | bytes 98336 | tf_op jit(solution)/shard_map/ppermute | solution.py:443
  59.6 3.0 %collective-permute-done.15.refs_5_ = bf16[4,48,256]{2,1,0:T(8,128)(2,1)S(1)} collective-permute-done((bf16[4,48,256]{2,1,0:T(8,128)(2,1)S(1)}, bf16[4,48,256]{2,1,0:T(8,128)(2,1)S(1)}, u32[]{:S(2)}, u32[]{:S(2)}) %collective-permute-start.15) | collective-permute-done | bytes 98336 | tf_op jit(solution)/shard_map/ppermute | solution.py:443
  62.6 1.2 %gather.1 = f32[4,8,48,256]{3,2,1,0:T(8,128)} custom-call(s32[1]{0:T(128)} %bitcast.refs_1_.me_ref, f32[4,48,256]{2,1,0:T(8,128)S(1)} %get-tuple-element.41.refs_0_, bf16[4,48,256]{2,1,0:T(8,128)(2,1)S(1)} %collective-permute-done.11.refs_1_, bf16[4,48,256]{2,1,0:T(8,128)(2,1)S(1)} %collective-permute-done.12.refs_2_, ...), custom_call_target="tpu_custom_call" | custom-call | tf_op jit(solution)/shard_map/gather/pallas_call | solution.py:445
  (42 shorter events, 9.9 us)
Async XLA Ops:
  1.0 4.6 %collective-permute-start = (f32[2,4,48,256]{3,2,1,0:T(8,128)S(1)}, f32[2,4,48,256]{3,2,1,0:T(8,128)S(1)}, u32[]{:S(2)}, u32[]{:S(2)}) collective-permute-start(f32[2,4,48,256]{3,2,1,0:T(8,128)S(1)} %dynamic-slice_bitcast_fusion), channel_id=1, source_target_pairs={{0,1},{1,0},{2,3},{3,2},{4,5},{5,4},{6,7},{7,6},{8,9},{9,8},{10,11... | collective-permute-start | bytes 1179656 | tf_op jit(solution)/shard_map/ppermute | solution.py:417
  1.7 1.4 %copy-start = (f32[1,2,2,8,48,256]{5,4,3,2,1,0:T(8,128)S(1)}, f32[1,2,2,8,48,256]{5,4,3,2,1,0:T(8,128)}, u32[]{:S(2)}) copy-start(f32[1,2,2,8,48,256]{5,4,3,2,1,0:T(8,128)} %param.5) | copy-start | bytes 4718596
  3.1 1.0 %copy-start.1 = (f32[8,48,256]{2,1,0:T(8,128)S(1)}, f32[8,48,256]{2,1,0:T(8,128)}, u32[]{:S(2)}) copy-start(f32[8,48,256]{2,1,0:T(8,128)} %refs_3_.1) | copy-start | bytes 1179652
  6.5 1.8 %collective-permute-start.1 = (f32[2,4,48,256]{3,2,1,0:T(8,128)S(1)}, f32[2,4,48,256]{3,2,1,0:T(8,128)S(1)}, u32[]{:S(2)}, u32[]{:S(2)}) collective-permute-start(f32[2,4,48,256]{3,2,1,0:T(8,128)S(1)} %get-tuple-element.28), channel_id=1, source_target_pairs={{0,1},{1,0},{2,3},{3,2},{4,5},{5,4},{6,7},{7,6},{8,9},{9,8},{10,11... | collective-permute-start | bytes 1179656 | tf_op jit(solution)/shard_map/ppermute | solution.py:417
  9.1 1.8 %collective-permute-start.2 = (f32[2,4,48,256]{3,2,1,0:T(8,128)S(1)}, f32[2,4,48,256]{3,2,1,0:T(8,128)S(1)}, u32[]{:S(2)}, u32[]{:S(2)}) collective-permute-start(f32[2,4,48,256]{3,2,1,0:T(8,128)S(1)} %get-tuple-element.30), channel_id=1, source_target_pairs={{0,1},{1,0},{2,3},{3,2},{4,5},{5,4},{6,7},{7,6},{8,9},{9,8},{10,11... | collective-permute-start | bytes 1179656 | tf_op jit(solution)/shard_map/ppermute | solution.py:417
  10.0 2.0 %copy-start.2 = (f32[8,48,256]{2,1,0:T(8,128)S(1)}, f32[8,48,256]{2,1,0:T(8,128)}, u32[]{:S(2)}) copy-start(f32[8,48,256]{2,1,0:T(8,128)} %refs_3_.1) | copy-start | bytes 1179652
  10.0 1.9 %copy-start.4 = (f32[1,4,8,256]{3,2,1,0:T(8,128)S(1)}, f32[1,4,8,256]{3,2,1,0:T(8,128)}, u32[]{:S(2)}) copy-start(f32[1,4,8,256]{3,2,1,0:T(8,128)} %param.6) | copy-start | bytes 98308
  11.7 1.8 %copy-start.5 = (s32[1,4]{1,0:T(1,128)S(1)}, s32[1,4]{1,0:T(1,128)}, u32[]{:S(2)}) copy-start(s32[1,4]{1,0:T(1,128)} %refs_2_.1) | copy-start | bytes 52
  11.7 1.8 %collective-permute-start.3 = (f32[2,4,48,256]{3,2,1,0:T(8,128)S(1)}, f32[2,4,48,256]{3,2,1,0:T(8,128)S(1)}, u32[]{:S(2)}, u32[]{:S(2)}) collective-permute-start(f32[2,4,48,256]{3,2,1,0:T(8,128)S(1)} %get-tuple-element.32), channel_id=1, source_target_pairs={{0,1},{1,0},{2,3},{3,2},{4,5},{5,4},{6,7},{7,6},{8,9},{9,8},{10,11... | collective-permute-start | bytes 1179656 | tf_op jit(solution)/shard_map/ppermute | solution.py:417
  13.5 21.8 %copy-start.6 = (s32[4]{0:T(128)S(1)}, s32[4]{0:T(128)}, u32[]{:S(2)}) copy-start(s32[4]{0:T(128)} %param.8) | copy-start | bytes 52
  14.9 11.0 %collective-permute-start.10 = (bf16[200,256]{1,0:T(8,128)(2,1)S(1)}, bf16[200,256]{1,0:T(8,128)(2,1)S(1)}, u32[]{:S(2)}, u32[]{:S(2)}) collective-permute-start(bf16[200,256]{1,0:T(8,128)(2,1)S(1)} %get-tuple-element.40), channel_id=1, source_target_pairs={{0,12},{2,14},{4,8},{6,10},{8,4},{10,6},{12,0},{14,2},{1,13},{3,15... | collective-permute-start | bytes 307208 | tf_op jit(solution)/shard_map/ppermute | solution.py:435
  19.7 14.1 %collective-permute-start.8 = (bf16[200,256]{1,0:T(8,128)(2,1)S(1)}, bf16[200,256]{1,0:T(8,128)(2,1)S(1)}, u32[]{:S(2)}, u32[]{:S(2)}) collective-permute-start(bf16[200,256]{1,0:T(8,128)(2,1)S(1)} %get-tuple-element.38), channel_id=1, source_target_pairs={{0,8},{2,10},{4,12},{6,14},{8,0},{10,2},{12,4},{14,6},{1,9},{3,11}... | collective-permute-start | bytes 307208 | tf_op jit(solution)/shard_map/ppermute | solution.py:435
  19.7 15.7 %collective-permute-start.9 = (bf16[200,256]{1,0:T(8,128)(2,1)S(1)}, bf16[200,256]{1,0:T(8,128)(2,1)S(1)}, u32[]{:S(2)}, u32[]{:S(2)}) collective-permute-start(bf16[200,256]{1,0:T(8,128)(2,1)S(1)} %get-tuple-element.39), channel_id=1, source_target_pairs={{0,14},{2,12},{4,10},{6,8},{8,6},{10,4},{12,2},{14,0},{1,15},{3,13... | collective-permute-start | bytes 307208 | tf_op jit(solution)/shard_map/ppermute | solution.py:435
  22.5 16.1 %collective-permute-start.4 = (bf16[200,256]{1,0:T(8,128)(2,1)S(1)}, bf16[200,256]{1,0:T(8,128)(2,1)S(1)}, u32[]{:S(2)}, u32[]{:S(2)}) collective-permute-start(bf16[200,256]{1,0:T(8,128)(2,1)S(1)} %get-tuple-element.33), channel_id=1, source_target_pairs={{0,10},{2,8},{4,14},{6,12},{8,2},{10,0},{12,6},{14,4},{1,11},{3,9}... | collective-permute-start | bytes 307208 | tf_op jit(solution)/shard_map/ppermute | solution.py:435
  23.5 15.1 %collective-permute-start.5 = (bf16[200,256]{1,0:T(8,128)(2,1)S(1)}, bf16[200,256]{1,0:T(8,128)(2,1)S(1)}, u32[]{:S(2)}, u32[]{:S(2)}) collective-permute-start(bf16[200,256]{1,0:T(8,128)(2,1)S(1)} %get-tuple-element.34), channel_id=1, source_target_pairs={{0,6},{2,4},{4,2},{6,0},{8,14},{10,12},{12,10},{14,8},{1,7},{3,5},... | collective-permute-start | bytes 307208 | tf_op jit(solution)/shard_map/ppermute | solution.py:435
  25.9 12.7 %collective-permute-start.6 = (bf16[200,256]{1,0:T(8,128)(2,1)S(1)}, bf16[200,256]{1,0:T(8,128)(2,1)S(1)}, u32[]{:S(2)}, u32[]{:S(2)}) collective-permute-start(bf16[200,256]{1,0:T(8,128)(2,1)S(1)} %get-tuple-element.35), channel_id=1, source_target_pairs={{0,4},{2,6},{4,0},{6,2},{8,12},{10,14},{12,8},{14,10},{1,5},{3,7},... | collective-permute-start | bytes 307208 | tf_op jit(solution)/shard_map/ppermute | solution.py:435
  33.8 5.9 %collective-permute-start.7 = (bf16[200,256]{1,0:T(8,128)(2,1)S(1)}, bf16[200,256]{1,0:T(8,128)(2,1)S(1)}, u32[]{:S(2)}, u32[]{:S(2)}) collective-permute-start(bf16[200,256]{1,0:T(8,128)(2,1)S(1)} %get-tuple-element.36), channel_id=1, source_target_pairs={{0,2},{2,0},{4,6},{6,4},{8,10},{10,8},{12,14},{14,12},{1,3},{3,1},... | collective-permute-start | bytes 307208 | tf_op jit(solution)/shard_map/ppermute | solution.py:435
  42.0 6.5 %collective-permute-start.11 = (bf16[4,48,256]{2,1,0:T(8,128)(2,1)S(1)}, bf16[4,48,256]{2,1,0:T(8,128)(2,1)S(1)}, u32[]{:S(2)}, u32[]{:S(2)}) collective-permute-start(bf16[4,48,256]{2,1,0:T(8,128)(2,1)S(1)} %get-tuple-element.42), channel_id=1, source_target_pairs={{0,2},{2,0},{4,6},{6,4},{8,10},{10,8},{12,14},{14,12},{1,3},{3,1},... | collective-permute-start | bytes 294920 | tf_op jit(solution)/shard_map/ppermute | solution.py:443
  42.7 8.4 %collective-permute-start.12 = (bf16[4,48,256]{2,1,0:T(8,128)(2,1)S(1)}, bf16[4,48,256]{2,1,0:T(8,128)(2,1)S(1)}, u32[]{:S(2)}, u32[]{:S(2)}) collective-permute-start(bf16[4,48,256]{2,1,0:T(8,128)(2,1)S(1)} %get-tuple-element.43), channel_id=1, source_target_pairs={{0,4},{2,6},{4,0},{6,2},{8,12},{10,14},{12,8},{14,10},{1,5},{3,7},... | collective-permute-start | bytes 294920 | tf_op jit(solution)/shard_map/ppermute | solution.py:443
  42.7 10.5 %collective-permute-start.13 = (bf16[4,48,256]{2,1,0:T(8,128)(2,1)S(1)}, bf16[4,48,256]{2,1,0:T(8,128)(2,1)S(1)}, u32[]{:S(2)}, u32[]{:S(2)}) collective-permute-start(bf16[4,48,256]{2,1,0:T(8,128)(2,1)S(1)} %get-tuple-element.44), channel_id=1, source_target_pairs={{0,6},{2,4},{4,2},{6,0},{8,14},{10,12},{12,10},{14,8},{1,7},{3,5},... | collective-permute-start | bytes 294920 | tf_op jit(solution)/shard_map/ppermute | solution.py:443
  45.6 14.0 %collective-permute-start.14 = (bf16[4,48,256]{2,1,0:T(8,128)(2,1)S(1)}, bf16[4,48,256]{2,1,0:T(8,128)(2,1)S(1)}, u32[]{:S(2)}, u32[]{:S(2)}) collective-permute-start(bf16[4,48,256]{2,1,0:T(8,128)(2,1)S(1)} %get-tuple-element.45), channel_id=1, source_target_pairs={{0,8},{2,10},{4,12},{6,14},{8,0},{10,2},{12,4},{14,6},{1,9},{3,11}... | collective-permute-start | bytes 294920 | tf_op jit(solution)/shard_map/ppermute | solution.py:443
  46.7 15.9 %collective-permute-start.15 = (bf16[4,48,256]{2,1,0:T(8,128)(2,1)S(1)}, bf16[4,48,256]{2,1,0:T(8,128)(2,1)S(1)}, u32[]{:S(2)}, u32[]{:S(2)}) collective-permute-start(bf16[4,48,256]{2,1,0:T(8,128)(2,1)S(1)} %get-tuple-element.46), channel_id=1, source_target_pairs={{0,10},{2,8},{4,14},{6,12},{8,2},{10,0},{12,6},{14,4},{1,11},{3,9}... | collective-permute-start | bytes 294920 | tf_op jit(solution)/shard_map/ppermute | solution.py:443
  48.5 14.0 %collective-permute-start.16 = (bf16[4,48,256]{2,1,0:T(8,128)(2,1)S(1)}, bf16[4,48,256]{2,1,0:T(8,128)(2,1)S(1)}, u32[]{:S(2)}, u32[]{:S(2)}) collective-permute-start(bf16[4,48,256]{2,1,0:T(8,128)(2,1)S(1)} %get-tuple-element.47), channel_id=1, source_target_pairs={{0,12},{2,14},{4,8},{6,10},{8,4},{10,6},{12,0},{14,2},{1,13},{3,15... | collective-permute-start | bytes 294920 | tf_op jit(solution)/shard_map/ppermute | solution.py:443
  51.1 11.5 %collective-permute-start.17 = (bf16[4,48,256]{2,1,0:T(8,128)(2,1)S(1)}, bf16[4,48,256]{2,1,0:T(8,128)(2,1)S(1)}, u32[]{:S(2)}, u32[]{:S(2)}) collective-permute-start(bf16[4,48,256]{2,1,0:T(8,128)(2,1)S(1)} %get-tuple-element.48), channel_id=1, source_target_pairs={{0,14},{2,12},{4,10},{6,8},{8,6},{10,4},{12,2},{14,0},{1,15},{3,13... | collective-permute-start | bytes 294920 | tf_op jit(solution)/shard_map/ppermute | solution.py:443
  (1 other events, 0.8 us)

commit v2 on v1

--- a/solution.py
+++ b/solution.py
@@ -161,7 +161,7 @@
         for t in range(tiles_x):
             across = pl.ds(t * LANES, LANES)
             at = (everything, across)
-            courant = courant_ref[y, :, across] * (BAND_UNIT / COMMON)
+            courant = courant_ref[y, :, across]
             for f in range(fields):
                 here = ext[f, i, t, pl.ds(SUBLANES, cells_z)]
                 lap = (3.0 * TAPS[0]) * here
@@ -379,7 +379,7 @@
 
 
 def far_first(groups):
-    order = (4, 5, 7, 3, 6, 2, 1)
+    order = (6, 7, 5, 4, 2, 3, 1)
     return [k for k in order if k < groups] + [k for k in range(8, groups)]
 
 
@@ -412,7 +412,8 @@
         (1, 1, fields, REACH, cells_z, cells_x),
     )[0, 0]
     earlier = current = None
-    constant = [courant_sq, traces[0], band]
+    drive = jnp.where(side >= 0, traces[0], 0.0)
+    constant = [courant_sq * (BAND_UNIT / COMMON), drive, band]
     for n in range(step_count):
         halo = lax.ppermute(edge, "gy", swap)
         last = n == step_count - 1
@@ -434,7 +435,7 @@
     for k in order:
         got[k] = lax.ppermute(parts[k], "off", pairs(k))
     offsets = groups * per_group
-    stages = ((0, 4, 7, 6), (5, 3, 2, 1))
+    stages = ((0, 6, 7, 1, 2), (5, 4, 3))
     images = None
     for i, ours in enumerate(stages):
         spec = (ours, groups, snaps, fields, i == 0, i == len(stages) - 1)

time: 64.7 us -> 62.8 us (0.971)
  local copies, waits for them, and re-layouts: 4.2 us -> 1.15 us
  other arithmetic: 0.16 us -> 1.96 us
  waiting for transfers between devices: 16.2 us -> 14.7 us
    unnamed x14 -> x6, local copies, waits for them, and re-layouts: 3.18 us -> 0.01 us
    ppermute x7, waiting for transfers between devices: 9.35 us -> 7.75 us  [on_device_planes(): back[k] = lax.ppermute(images[k], 'off', pairs(k))]
    mul x0 -> x1, other arithmetic: none -> 1.03 us  [on_device_planes(): constant = [courant_sq * (BAND_UNIT / COMMON), drive, band]]
    select_n x0 -> x1, other arithmetic: none -> 0.76 us  [on_device_planes(): drive = jnp.where(side >= 0, traces[0], 0.0)]
  transfers between devices with their start and end apart: 18 -> 18, of which waited for: 8 -> 8; matrix products, arithmetic and copies ran while one was open for 0% -> 3% of each run, Pallas kernels for 7% -> 8%
where the time goes in v2:
time: 62.8 us; the launch traced here: 61.8 us
  starting transfers between devices  31.5 us (50%)
  waiting for transfers between devices  14.7 us (23%)
  Pallas kernels  12.4 us (20%)
  other arithmetic  1.96 us (3%)
  local copies, waits for them, and re-layouts  1.15 us (2%)
    ppermute x7, starting transfers between devices, on_device_planes(): got[k] = lax.ppermute(parts[k], 'off', pairs(k))  19.3 us
    ppermute x7, starting transfers between devices, on_device_planes(): back[k] = lax.ppermute(images[k], 'off', pairs(k))  11.2 us
    ppermute x7, waiting for transfers between devices, on_device_planes(): back[k] = lax.ppermute(images[k], 'off', pairs(k))  7.75 us
    pallas_call x8, Pallas kernels, half_step(): pl.pallas_call(kernel, out_shape=outs, in_specs=[SMEM] * scalars + [VMEM]...  6.9 us
    pallas_call x2, Pallas kernels, imaged(): pl.pallas_call(functools.partial(image_kernel, spec), out_shape=outs, in_...  4.23 us
    ppermute x7, waiting for transfers between devices, on_device_planes(): got[k] = lax.ppermute(parts[k], 'off', pairs(k))  3.81 us
    ppermute x4, waiting for transfers between devices, on_device_planes(): halo = lax.ppermute(edge, 'gy', swap)  3.13 us
  transfers between devices with their start and end apart: 18, of which 8 were waited for; matrix products, arithmetic and copies ran while one was open for 3% of the time, Pallas kernels for 8%

profile of v2, /device:TPU:0, one launch (start us, length us, event | category | flops | bytes accessed | tf_op | source)
XLA Modules:
  0.0 61.8 jit_solution(18030056133020665769)
XLA Ops:
  0.0 1.1 %dynamic-slice_bitcast_fusion = f32[2,4,48,256]{3,2,1,0:T(8,128)S(1)} fusion(f32[1,2,2,8,48,256]{5,4,3,2,1,0:T(8,128)} %param.5, s32[]{:T(128)S(6)} %select_n.89), kind=kLoop, calls=%fused_computation | loop fusion | bytes 786436 | tf_op jit(solution)/shard_map/squeeze | solution.py:409
  2.5 1.0 %broadcast_multiply_fusion.refs_1_.refs_3_ = f32[8,48,256]{2,1,0:T(8,128)S(1)} fusion(f32[8,48,256]{2,1,0:T(8,128)} %param.7), kind=kLoop, calls=%fused_computation.7 | loop fusion | flops 98304 | bytes 786432 | tf_op jit(solution)/shard_map/mul | solution.py:416
  5.7 1.0 %collective-permute-done.1.refs_6_ = f32[2,4,48,256]{3,2,1,0:T(8,128)S(1)} collective-permute-done((f32[2,4,48,256]{3,2,1,0:T(8,128)S(1)}, f32[2,4,48,256]{3,2,1,0:T(8,128)S(1)}, u32[]{:S(2)}, u32[]{:S(2)}) %collective-permute-start.1) | collective-permute-done | bytes 393248 | tf_op jit(solution)/shard_map/ppermute | solution.py:418
  9.3 1.5 %near.6 = (f32[2,8,48,256]{3,2,1,0:T(8,128)S(1)}, f32[2,4,48,256]{3,2,1,0:T(8,128)}) custom-call(s32[1]{0:T(128)} %bitcast.1.refs_0_, f32[8,48,256]{2,1,0:T(8,128)S(1)} %broadcast_multiply_fusion.refs_1_.refs_3_, f32[4,8,256]{2,1,0:T(8,128)S(1)} %select_bitcast_fusion.refs_2_.refs_4_, bf16[256,256]{1,0:T(8,128)(2,1)S(1)} %select_convert_fusion.refs_3_.refs_5_, ...), custom_call_target="tpu_custom_call" | custom-call | flops 196608000 | bytes 1572864 | tf_op jit(solution)/shard_map/near/pallas_call | solution.py:229
  11.6 1.2 %collective-permute-done.3.refs_8_ = f32[2,4,48,256]{3,2,1,0:T(8,128)S(1)} collective-permute-done((f32[2,4,48,256]{3,2,1,0:T(8,128)}, f32[2,4,48,256]{3,2,1,0:T(8,128)S(1)}, u32[]{:S(2)}, u32[]{:S(2)}) %collective-permute-start.3) | collective-permute-done | bytes 393248 | tf_op jit(solution)/shard_map/ppermute | solution.py:418
  12.8 1.3 %near.7 = (bf16[200,256]{1,0:T(8,128)(2,1)S(1)}, bf16[200,256]{1,0:T(8,128)(2,1)S(1)}, bf16[200,256]{1,0:T(8,128)(2,1)S(1)}, bf16[200,256]{1,0:T(8,128)(2,1)S(1)...) custom-call(s32[1]{0:T(128)} %bitcast.1.refs_0_, ...), custom_call_target="tpu_custom_call" | custom-call | flops 196608000 | bytes 1572864 | tf_op jit(solution)/shard_map/near/pallas_call | solution.py:229
  14.1 2.8 %collective-permute-start.10 = (bf16[200,256]{1,0:T(8,128)(2,1)S(1)}, bf16[200,256]{1,0:T(8,128)(2,1)S(1)}, u32[]{:S(2)}, u32[]{:S(2)}) collective-permute-start(bf16[200,256]{1,0:T(8,128)(2,1)S(1)} %get-tuple-element.40), channel_id=1, source_target_pairs={{0,4},{2,6},{4,0},{6,2},{8,12},{10,14},{12,8},{14,10},{1,5},{3,7},... | collective-permute-start | bytes 307208 | tf_op jit(solution)/shard_map/ppermute | solution.py:436
  16.9 2.5 %collective-permute-start.7 = (bf16[200,256]{1,0:T(8,128)(2,1)S(1)}, bf16[200,256]{1,0:T(8,128)(2,1)S(1)}, u32[]{:S(2)}, u32[]{:S(2)}) collective-permute-start(bf16[200,256]{1,0:T(8,128)(2,1)S(1)} %get-tuple-element.37), channel_id=1, source_target_pairs={{0,12},{2,14},{4,8},{6,10},{8,4},{10,6},{12,0},{14,2},{1,13},{3,15... | collective-permute-start | bytes 307208 | tf_op jit(solution)/shard_map/ppermute | solution.py:436
  19.3 2.3 %collective-permute-start.8 = (bf16[200,256]{1,0:T(8,128)(2,1)S(1)}, bf16[200,256]{1,0:T(8,128)(2,1)S(1)}, u32[]{:S(2)}, u32[]{:S(2)}) collective-permute-start(bf16[200,256]{1,0:T(8,128)(2,1)S(1)} %get-tuple-element.38), channel_id=1, source_target_pairs={{0,14},{2,12},{4,10},{6,8},{8,6},{10,4},{12,2},{14,0},{1,15},{3,13... | collective-permute-start | bytes 307208 | tf_op jit(solution)/shard_map/ppermute | solution.py:436
  22.2 1.7 %collective-permute-start.4 = (bf16[200,256]{1,0:T(8,128)(2,1)S(1)}, bf16[200,256]{1,0:T(8,128)(2,1)S(1)}, u32[]{:S(2)}, u32[]{:S(2)}) collective-permute-start(bf16[200,256]{1,0:T(8,128)(2,1)S(1)} %get-tuple-element.33), channel_id=1, source_target_pairs={{0,10},{2,8},{4,14},{6,12},{8,2},{10,0},{12,6},{14,4},{1,11},{3,9}... | collective-permute-start | bytes 307208 | tf_op jit(solution)/shard_map/ppermute | solution.py:436
  23.9 2.1 %collective-permute-start.5 = (bf16[200,256]{1,0:T(8,128)(2,1)S(1)}, bf16[200,256]{1,0:T(8,128)(2,1)S(1)}, u32[]{:S(2)}, u32[]{:S(2)}) collective-permute-start(bf16[200,256]{1,0:T(8,128)(2,1)S(1)} %get-tuple-element.34), channel_id=1, source_target_pairs={{0,8},{2,10},{4,12},{6,14},{8,0},{10,2},{12,4},{14,6},{1,9},{3,11}... | collective-permute-start | bytes 307208 | tf_op jit(solution)/shard_map/ppermute | solution.py:436
  26.0 7.4 %collective-permute-start.6 = (bf16[200,256]{1,0:T(8,128)(2,1)S(1)}, bf16[200,256]{1,0:T(8,128)(2,1)S(1)}, u32[]{:S(2)}, u32[]{:S(2)}) collective-permute-start(bf16[200,256]{1,0:T(8,128)(2,1)S(1)} %get-tuple-element.35), channel_id=1, source_target_pairs={{0,6},{2,4},{4,2},{6,0},{8,14},{10,12},{12,10},{14,8},{1,7},{3,5},... | collective-permute-start | bytes 307208 | tf_op jit(solution)/shard_map/ppermute | solution.py:436
  33.6 2.6 %image.2.refs_3_ = f32[32,48,256]{2,1,0:T(8,128)S(1)} custom-call(s32[8]{0:T(128)S(1)} %convert_element_type.20.valid_ref, bf16[200,256]{1,0:T(8,128)(2,1)S(1)} %get-tuple-element.36.refs_0_.refs_4_, bf16[200,256]{1,0:T(8,128)(2,1)S(1)} %collective-permute-done.7.refs_1_.refs_10_, bf16[200,256]{1,0:T(8,128)(2,1)S(1)} %collective-permute-done.8.refs_2_.refs_11_, ...), custom_call_target="tpu_custom_call" | custom-call | flops 786432000 | bytes 3145728 | tf_op jit(solution)/shard_map/image/pallas_call | solution.py:351
  36.1 1.3 %collective-permute-done.4.refs_0_.refs_9_ = bf16[200,256]{1,0:T(8,128)(2,1)S(1)} collective-permute-done((bf16[200,256]{1,0:T(8,128)(2,1)S(1)}, bf16[200,256]{1,0:T(8,128)(2,1)S(1)}, u32[]{:S(2)}, u32[]{:S(2)}) %collective-permute-start.4) | collective-permute-done | bytes 102432 | tf_op jit(solution)/shard_map/ppermute | solution.py:436
  38.1 1.9 %collective-permute-done.6.refs_2_.refs_7_ = bf16[200,256]{1,0:T(8,128)(2,1)S(1)} collective-permute-done((bf16[200,256]{1,0:T(8,128)(2,1)S(1)}, bf16[200,256]{1,0:T(8,128)(2,1)S(1)}, u32[]{:S(2)}, u32[]{:S(2)}) %collective-permute-start.6) | collective-permute-done | bytes 102432 | tf_op jit(solution)/shard_map/ppermute | solution.py:436
  39.9 1.7 %image.3 = (f32[4,48,256]{2,1,0:T(8,128)S(1)}, bf16[4,48,256]{2,1,0:T(8,128)(2,1)S(1)}, bf16[4,48,256]{2,1,0:T(8,128)(2,1)S(1)}, bf16[4,48,256]{2,1,0:T(8,128)(2...) custom-call(s32[8]{0:T(128)S(1)} %convert_element_type.20.valid_ref,, ...), custom_call_target="tpu_custom_call" | custom-call | flops 471859200 | bytes 3145728 | tf_op jit(solution)/shard_map/image/pallas_call | solution.py:351
  42.4 2.8 %collective-permute-start.13 = (bf16[4,48,256]{2,1,0:T(8,128)(2,1)S(1)}, bf16[4,48,256]{2,1,0:T(8,128)(2,1)S(1)}, u32[]{:S(2)}, u32[]{:S(2)}) collective-permute-start(bf16[4,48,256]{2,1,0:T(8,128)(2,1)S(1)} %get-tuple-element.44), channel_id=1, source_target_pairs={{0,6},{2,4},{4,2},{6,0},{8,14},{10,12},{12,10},{14,8},{1,7},{3,5},... | collective-permute-start | bytes 294920 | tf_op jit(solution)/shard_map/ppermute | solution.py:444
  45.2 1.2 %collective-permute-start.14 = (bf16[4,48,256]{2,1,0:T(8,128)(2,1)S(1)}, bf16[4,48,256]{2,1,0:T(8,128)(2,1)S(1)}, u32[]{:S(2)}, u32[]{:S(2)}) collective-permute-start(bf16[4,48,256]{2,1,0:T(8,128)(2,1)S(1)} %get-tuple-element.45), channel_id=1, source_target_pairs={{0,8},{2,10},{4,12},{6,14},{8,0},{10,2},{12,4},{14,6},{1,9},{3,11}... | collective-permute-start | bytes 294920 | tf_op jit(solution)/shard_map/ppermute | solution.py:444
  46.3 1.7 %collective-permute-start.15 = (bf16[4,48,256]{2,1,0:T(8,128)(2,1)S(1)}, bf16[4,48,256]{2,1,0:T(8,128)(2,1)S(1)}, u32[]{:S(2)}, u32[]{:S(2)}) collective-permute-start(bf16[4,48,256]{2,1,0:T(8,128)(2,1)S(1)} %get-tuple-element.46), channel_id=1, source_target_pairs={{0,10},{2,8},{4,14},{6,12},{8,2},{10,0},{12,6},{14,4},{1,11},{3,9}... | collective-permute-start | bytes 294920 | tf_op jit(solution)/shard_map/ppermute | solution.py:444
  48.1 2.2 %collective-permute-start.16 = (bf16[4,48,256]{2,1,0:T(8,128)(2,1)S(1)}, bf16[4,48,256]{2,1,0:T(8,128)(2,1)S(1)}, u32[]{:S(2)}, u32[]{:S(2)}) collective-permute-start(bf16[4,48,256]{2,1,0:T(8,128)(2,1)S(1)} %get-tuple-element.47), channel_id=1, source_target_pairs={{0,12},{2,14},{4,8},{6,10},{8,4},{10,6},{12,0},{14,2},{1,13},{3,15... | collective-permute-start | bytes 294920 | tf_op jit(solution)/shard_map/ppermute | solution.py:444
  50.3 2.6 %collective-permute-start.17 = (bf16[4,48,256]{2,1,0:T(8,128)(2,1)S(1)}, bf16[4,48,256]{2,1,0:T(8,128)(2,1)S(1)}, u32[]{:S(2)}, u32[]{:S(2)}) collective-permute-start(bf16[4,48,256]{2,1,0:T(8,128)(2,1)S(1)} %get-tuple-element.48), channel_id=1, source_target_pairs={{0,14},{2,12},{4,10},{6,8},{8,6},{10,4},{12,2},{14,0},{1,15},{3,13... | collective-permute-start | bytes 294920 | tf_op jit(solution)/shard_map/ppermute | solution.py:444
  52.8 4.2 %collective-permute-done.14.refs_4_ = bf16[4,48,256]{2,1,0:T(8,128)(2,1)S(1)} collective-permute-done((bf16[4,48,256]{2,1,0:T(8,128)(2,1)S(1)}, bf16[4,48,256]{2,1,0:T(8,128)(2,1)S(1)}, u32[]{:S(2)}, u32[]{:S(2)}) %collective-permute-start.14) | collective-permute-done | bytes 98336 | tf_op jit(solution)/shard_map/ppermute | solution.py:444
  57.0 3.6 %collective-permute-done.15.refs_5_ = bf16[4,48,256]{2,1,0:T(8,128)(2,1)S(1)} collective-permute-done((bf16[4,48,256]{2,1,0:T(8,128)(2,1)S(1)}, bf16[4,48,256]{2,1,0:T(8,128)(2,1)S(1)}, u32[]{:S(2)}, u32[]{:S(2)}) %collective-permute-start.15) | collective-permute-done | bytes 98336 | tf_op jit(solution)/shard_map/ppermute | solution.py:444
  60.6 1.2 %gather.1 = f32[4,8,48,256]{3,2,1,0:T(8,128)} custom-call(s32[1]{0:T(128)} %bitcast.refs_1_.me_ref, f32[4,48,256]{2,1,0:T(8,128)S(1)} %get-tuple-element.41.refs_0_, bf16[4,48,256]{2,1,0:T(8,128)(2,1)S(1)} %collective-permute-done.11.refs_1_, bf16[4,48,256]{2,1,0:T(8,128)(2,1)S(1)} %collective-permute-done.12.refs_2_, ...), custom_call_target="tpu_custom_call" | custom-call | tf_op jit(solution)/shard_map/gather/pallas_call | solution.py:446
  (36 shorter events, 9.0 us)
Async XLA Ops:
  0.0 3.6 %copy-start = (f32[1,2,2,8,48,256]{5,4,3,2,1,0:T(8,128)S(1)}, f32[1,2,2,8,48,256]{5,4,3,2,1,0:T(8,128)}, u32[]{:S(2)}) copy-start(f32[1,2,2,8,48,256]{5,4,3,2,1,0:T(8,128)} %param.5) | copy-start | bytes 4718596
  1.1 3.1 %collective-permute-start = (f32[2,4,48,256]{3,2,1,0:T(8,128)S(1)}, f32[2,4,48,256]{3,2,1,0:T(8,128)S(1)}, u32[]{:S(2)}, u32[]{:S(2)}) collective-permute-start(f32[2,4,48,256]{3,2,1,0:T(8,128)S(1)} %dynamic-slice_bitcast_fusion), channel_id=1, source_target_pairs={{0,1},{1,0},{2,3},{3,2},{4,5},{5,4},{6,7},{7,6},{8,9},{9,8},{10,11... | collective-permute-start | bytes 1179656 | tf_op jit(solution)/shard_map/ppermute | solution.py:418
  4.9 1.8 %collective-permute-start.1 = (f32[2,4,48,256]{3,2,1,0:T(8,128)S(1)}, f32[2,4,48,256]{3,2,1,0:T(8,128)S(1)}, u32[]{:S(2)}, u32[]{:S(2)}) collective-permute-start(f32[2,4,48,256]{3,2,1,0:T(8,128)S(1)} %get-tuple-element.28), channel_id=1, source_target_pairs={{0,1},{1,0},{2,3},{3,2},{4,5},{5,4},{6,7},{7,6},{8,9},{9,8},{10,11... | collective-permute-start | bytes 1179656 | tf_op jit(solution)/shard_map/ppermute | solution.py:418
  7.5 1.8 %collective-permute-start.2 = (f32[2,4,48,256]{3,2,1,0:T(8,128)S(1)}, f32[2,4,48,256]{3,2,1,0:T(8,128)S(1)}, u32[]{:S(2)}, u32[]{:S(2)}) collective-permute-start(f32[2,4,48,256]{3,2,1,0:T(8,128)S(1)} %get-tuple-element.30), channel_id=1, source_target_pairs={{0,1},{1,0},{2,3},{3,2},{4,5},{5,4},{6,7},{7,6},{8,9},{9,8},{10,11... | collective-permute-start | bytes 1179656 | tf_op jit(solution)/shard_map/ppermute | solution.py:418
  10.9 1.9 %copy-start.1 = (s32[1,4]{1,0:T(1,128)S(1)}, s32[1,4]{1,0:T(1,128)}, u32[]{:S(2)}) copy-start(s32[1,4]{1,0:T(1,128)} %refs_2_.1) | copy-start | bytes 52
  10.9 1.9 %collective-permute-start.3 = (f32[2,4,48,256]{3,2,1,0:T(8,128)}, f32[2,4,48,256]{3,2,1,0:T(8,128)S(1)}, u32[]{:S(2)}, u32[]{:S(2)}) collective-permute-start(f32[2,4,48,256]{3,2,1,0:T(8,128)} %get-tuple-element.32), channel_id=1, source_target_pairs={{0,1},{1,0},{2,3},{3,2},{4,5},{5,4},{6,7},{7,6},{8,9},{9,8},{10,11... | collective-permute-start | bytes 1179656 | tf_op jit(solution)/shard_map/ppermute | solution.py:418
  12.8 20.7 %copy-start.2 = (s32[4]{0:T(128)S(1)}, s32[4]{0:T(128)}, u32[]{:S(2)}) copy-start(s32[4]{0:T(128)} %param.8) | copy-start | bytes 52
  14.1 9.8 %collective-permute-start.10 = (bf16[200,256]{1,0:T(8,128)(2,1)S(1)}, bf16[200,256]{1,0:T(8,128)(2,1)S(1)}, u32[]{:S(2)}, u32[]{:S(2)}) collective-permute-start(bf16[200,256]{1,0:T(8,128)(2,1)S(1)} %get-tuple-element.40), channel_id=1, source_target_pairs={{0,4},{2,6},{4,0},{6,2},{8,12},{10,14},{12,8},{14,10},{1,5},{3,7},... | collective-permute-start | bytes 307208 | tf_op jit(solution)/shard_map/ppermute | solution.py:436
  16.9 9.2 %collective-permute-start.7 = (bf16[200,256]{1,0:T(8,128)(2,1)S(1)}, bf16[200,256]{1,0:T(8,128)(2,1)S(1)}, u32[]{:S(2)}, u32[]{:S(2)}) collective-permute-start(bf16[200,256]{1,0:T(8,128)(2,1)S(1)} %get-tuple-element.37), channel_id=1, source_target_pairs={{0,12},{2,14},{4,8},{6,10},{8,4},{10,6},{12,0},{14,2},{1,13},{3,15... | collective-permute-start | bytes 307208 | tf_op jit(solution)/shard_map/ppermute | solution.py:436
  19.3 14.2 %collective-permute-start.8 = (bf16[200,256]{1,0:T(8,128)(2,1)S(1)}, bf16[200,256]{1,0:T(8,128)(2,1)S(1)}, u32[]{:S(2)}, u32[]{:S(2)}) collective-permute-start(bf16[200,256]{1,0:T(8,128)(2,1)S(1)} %get-tuple-element.38), channel_id=1, source_target_pairs={{0,14},{2,12},{4,10},{6,8},{8,6},{10,4},{12,2},{14,0},{1,15},{3,13... | collective-permute-start | bytes 307208 | tf_op jit(solution)/shard_map/ppermute | solution.py:436
  21.6 11.9 %collective-permute-start.9 = (bf16[200,256]{1,0:T(8,128)(2,1)S(1)}, bf16[200,256]{1,0:T(8,128)(2,1)S(1)}, u32[]{:S(2)}, u32[]{:S(2)}) collective-permute-start(bf16[200,256]{1,0:T(8,128)(2,1)S(1)} %get-tuple-element.39), channel_id=1, source_target_pairs={{0,2},{2,0},{4,6},{6,4},{8,10},{10,8},{12,14},{14,12},{1,3},{3,1},... | collective-permute-start | bytes 307208 | tf_op jit(solution)/shard_map/ppermute | solution.py:436
  22.2 15.2 %collective-permute-start.4 = (bf16[200,256]{1,0:T(8,128)(2,1)S(1)}, bf16[200,256]{1,0:T(8,128)(2,1)S(1)}, u32[]{:S(2)}, u32[]{:S(2)}) collective-permute-start(bf16[200,256]{1,0:T(8,128)(2,1)S(1)} %get-tuple-element.33), channel_id=1, source_target_pairs={{0,10},{2,8},{4,14},{6,12},{8,2},{10,0},{12,6},{14,4},{1,11},{3,9}... | collective-permute-start | bytes 307208 | tf_op jit(solution)/shard_map/ppermute | solution.py:436
  23.9 14.2 %collective-permute-start.5 = (bf16[200,256]{1,0:T(8,128)(2,1)S(1)}, bf16[200,256]{1,0:T(8,128)(2,1)S(1)}, u32[]{:S(2)}, u32[]{:S(2)}) collective-permute-start(bf16[200,256]{1,0:T(8,128)(2,1)S(1)} %get-tuple-element.34), channel_id=1, source_target_pairs={{0,8},{2,10},{4,12},{6,14},{8,0},{10,2},{12,4},{14,6},{1,9},{3,11}... | collective-permute-start | bytes 307208 | tf_op jit(solution)/shard_map/ppermute | solution.py:436
  26.0 13.9 %collective-permute-start.6 = (bf16[200,256]{1,0:T(8,128)(2,1)S(1)}, bf16[200,256]{1,0:T(8,128)(2,1)S(1)}, u32[]{:S(2)}, u32[]{:S(2)}) collective-permute-start(bf16[200,256]{1,0:T(8,128)(2,1)S(1)} %get-tuple-element.35), channel_id=1, source_target_pairs={{0,6},{2,4},{4,2},{6,0},{8,14},{10,12},{12,10},{14,8},{1,7},{3,5},... | collective-permute-start | bytes 307208 | tf_op jit(solution)/shard_map/ppermute | solution.py:436
  41.6 6.5 %collective-permute-start.11 = (bf16[4,48,256]{2,1,0:T(8,128)(2,1)S(1)}, bf16[4,48,256]{2,1,0:T(8,128)(2,1)S(1)}, u32[]{:S(2)}, u32[]{:S(2)}) collective-permute-start(bf16[4,48,256]{2,1,0:T(8,128)(2,1)S(1)} %get-tuple-element.42), channel_id=1, source_target_pairs={{0,2},{2,0},{4,6},{6,4},{8,10},{10,8},{12,14},{14,12},{1,3},{3,1},... | collective-permute-start | bytes 294920 | tf_op jit(solution)/shard_map/ppermute | solution.py:444
  42.2 8.0 %collective-permute-start.12 = (bf16[4,48,256]{2,1,0:T(8,128)(2,1)S(1)}, bf16[4,48,256]{2,1,0:T(8,128)(2,1)S(1)}, u32[]{:S(2)}, u32[]{:S(2)}) collective-permute-start(bf16[4,48,256]{2,1,0:T(8,128)(2,1)S(1)} %get-tuple-element.43), channel_id=1, source_target_pairs={{0,4},{2,6},{4,0},{6,2},{8,12},{10,14},{12,8},{14,10},{1,5},{3,7},... | collective-permute-start | bytes 294920 | tf_op jit(solution)/shard_map/ppermute | solution.py:444
  42.4 10.4 %collective-permute-start.13 = (bf16[4,48,256]{2,1,0:T(8,128)(2,1)S(1)}, bf16[4,48,256]{2,1,0:T(8,128)(2,1)S(1)}, u32[]{:S(2)}, u32[]{:S(2)}) collective-permute-start(bf16[4,48,256]{2,1,0:T(8,128)(2,1)S(1)} %get-tuple-element.44), channel_id=1, source_target_pairs={{0,6},{2,4},{4,2},{6,0},{8,14},{10,12},{12,10},{14,8},{1,7},{3,5},... | collective-permute-start | bytes 294920 | tf_op jit(solution)/shard_map/ppermute | solution.py:444
  45.2 11.8 %collective-permute-start.14 = (bf16[4,48,256]{2,1,0:T(8,128)(2,1)S(1)}, bf16[4,48,256]{2,1,0:T(8,128)(2,1)S(1)}, u32[]{:S(2)}, u32[]{:S(2)}) collective-permute-start(bf16[4,48,256]{2,1,0:T(8,128)(2,1)S(1)} %get-tuple-element.45), channel_id=1, source_target_pairs={{0,8},{2,10},{4,12},{6,14},{8,0},{10,2},{12,4},{14,6},{1,9},{3,11}... | collective-permute-start | bytes 294920 | tf_op jit(solution)/shard_map/ppermute | solution.py:444
  46.3 14.2 %collective-permute-start.15 = (bf16[4,48,256]{2,1,0:T(8,128)(2,1)S(1)}, bf16[4,48,256]{2,1,0:T(8,128)(2,1)S(1)}, u32[]{:S(2)}, u32[]{:S(2)}) collective-permute-start(bf16[4,48,256]{2,1,0:T(8,128)(2,1)S(1)} %get-tuple-element.46), channel_id=1, source_target_pairs={{0,10},{2,8},{4,14},{6,12},{8,2},{10,0},{12,6},{14,4},{1,11},{3,9}... | collective-permute-start | bytes 294920 | tf_op jit(solution)/shard_map/ppermute | solution.py:444
  48.1 12.5 %collective-permute-start.16 = (bf16[4,48,256]{2,1,0:T(8,128)(2,1)S(1)}, bf16[4,48,256]{2,1,0:T(8,128)(2,1)S(1)}, u32[]{:S(2)}, u32[]{:S(2)}) collective-permute-start(bf16[4,48,256]{2,1,0:T(8,128)(2,1)S(1)} %get-tuple-element.47), channel_id=1, source_target_pairs={{0,12},{2,14},{4,8},{6,10},{8,4},{10,6},{12,0},{14,2},{1,13},{3,15... | collective-permute-start | bytes 294920 | tf_op jit(solution)/shard_map/ppermute | solution.py:444
  50.3 10.3 %collective-permute-start.17 = (bf16[4,48,256]{2,1,0:T(8,128)(2,1)S(1)}, bf16[4,48,256]{2,1,0:T(8,128)(2,1)S(1)}, u32[]{:S(2)}, u32[]{:S(2)}) collective-permute-start(bf16[4,48,256]{2,1,0:T(8,128)(2,1)S(1)} %get-tuple-element.48), channel_id=1, source_target_pairs={{0,14},{2,12},{4,10},{6,8},{8,6},{10,4},{12,2},{14,0},{1,15},{3,13... | collective-permute-start | bytes 294920 | tf_op jit(solution)/shard_map/ppermute | solution.py:444
